TPU v7x, 32 devices: a whole 2x2x4 slice. The times are simulated.
32 devices in a mesh: depth: 4 (over x, core), tile: 8 (over z, y).
Axes of the slice: x: 2, y: 2, z: 4, core: 2. Of those that a mesh axis runs over, the one named last changes fastest.
Arguments:
- volume: bfloat16 [512, 64, 64, 64], P(('depth', 'tile')), may hold values from 0.0099487305 to 0.5
- resampler: bfloat16 [2, 64, 128], replicated, may hold values from 0 to 1.4, as said below
- ramp_slope: float32 [3], replicated, may hold values from -12 to 12
- ramp_pivot: float32 [3], replicated, may hold values from 0.03 to 0.3
- tile_owner: int32 [512, 2], P(('depth', 'tile')), may hold values from 0 to 7, all different within a row; in each aligned block of 16 rows (0 to 15, 16 to 31, ...) at most 8 rows name the same one
- tile_cell: int32 [512, 2], P(('depth', 'tile')), may hold values from 0 to 7
- depth_order: int32 [2, 512], P(None, ('depth', 'tile')), may hold values from 0 to 511, each once within a row
- slab_rank: int32 [2, 4], replicated, may hold values from 0 to 3, each once within a row
Outputs:
- colour: float32 [2, 3, 8, 512, 128], P(None, None, 'tile', 'depth')
- transmittance: float32 [2, 8, 512, 128], P(None, 'tile', 'depth')
Inputs may be any that keep to these rules, and one draw needn't show every extreme that they name: `tile_owner`: each row names 2 different tile owners. Among the 16 rows of one device no owner is named by more than 8 rows, a bound that some block reaches. `depth_order`: each row is a permutation. `slab_rank`: each row is a permutation. `resampler`: nonnegative interpolation weights.
All inputs are finite; a program needn't handle non-finite values.
Results may differ from a plain program's by a relative error of at most 0.0025.
Values may be sent and summed in bfloat16 or wider, within the bound.
No kernel may reach another device: no remote copies, remote signals or barrier semaphores. Data moves between devices by JAX's collectives and lax.ppermute only.
A program may use at most 128 MiB of HBM per device.

v0:
```python
import jax
import jax.numpy as jnp
from jax import lax
from jax.sharding import PartitionSpec as P

CELLS = 8


EXTINCTION = 1.0
TOP_PRECISION = lax.Precision.HIGHEST


def render_brick(brick, resampler, strict_lower, ramp_slope, ramp_pivot):
    rowwise_axis = jnp.einsum(
        "kri,is->krs", brick, resampler[0], preferred_element_type=jnp.float32
    )
    along_depth = jnp.einsum("rik,is->krs", brick, resampler[1], preferred_element_type=jnp.float32)
    samples = jnp.stack([rowwise_axis, along_depth])
    optical = samples * (EXTINCTION / samples.shape[1])
    nearest_depth = jnp.einsum("kj,vjrs->vkrs", strict_lower, optical, precision=TOP_PRECISION)
    weight = jnp.exp(-nearest_depth) * (1.0 - jnp.exp(-optical))
    layers = []
    for channel in range(3):
        tinted = jax.nn.sigmoid(ramp_slope[channel] * (samples - ramp_pivot[channel]))
        layers.append(jnp.sum(weight * tinted, axis=1))
    layers.append(jnp.sum(optical, axis=1))
    return jnp.stack(layers, axis=1)


def bucket_slots(targets):
    positions = jnp.arange(targets.shape[0])
    earlier = (targets[None, :] == targets[:, None]) & (positions[None, :] < positions[:, None])
    return jnp.sum(earlier.astype(jnp.int32), axis=1)


def compose(received, filled, view_tag, cell_tag, rank_tag, view_count):
    slot_count, _, brick_rows, sample_cols = received.shape
    before = filled[None, :] & (view_tag[None, :] == view_tag[:, None])
    before = (
        before & (cell_tag[None, :] == cell_tag[:, None]) & (rank_tag[None, :] < rank_tag[:, None])
    )
    depth_values = received[:, 3].reshape(slot_count, brick_rows * sample_cols)
    nearest_depth = jnp.dot(before.astype(jnp.float32), depth_values, precision=TOP_PRECISION)
    nearest_depth = nearest_depth.reshape(slot_count, brick_rows, sample_cols)
    lit_colour = received[:, :3] * jnp.exp(-nearest_depth)[:, None]
    view_ids = jnp.arange(view_count, dtype=jnp.int32)
    cell_ids = jnp.arange(CELLS, dtype=jnp.int32)
    selector = filled[None, None, :] & (view_tag[None, None, :] == view_ids[:, None, None])
    selector = (selector & (cell_tag[None, None, :] == cell_ids[None, :, None])).astype(jnp.float32)
    colour = jnp.einsum("vcq,qxrw->vxcrw", selector, lit_colour, precision=TOP_PRECISION)
    optical_total = jnp.einsum("vcq,qrw->vcrw", selector, received[:, 3], precision=TOP_PRECISION)
    tile_rows = CELLS * brick_rows
    colour = colour.reshape(view_count, 3, tile_rows, sample_cols)
    optical_total = optical_total.reshape(view_count, 1, tile_rows, sample_cols)
    return jnp.concatenate([colour, optical_total], axis=1).astype(jnp.bfloat16)


def blend_slabs(stacked, slab_rank):
    is_nearer = (slab_rank[:, None, :] < slab_rank[:, :, None]).astype(jnp.float32)
    depth_values = stacked[:, :, 3]
    nearest_depth = jnp.einsum("ksz,zkoh->skoh", is_nearer, depth_values, precision=TOP_PRECISION)
    colour = jnp.sum(jnp.exp(-nearest_depth)[:, :, None] * stacked[:, :, :3], axis=0)
    transmit = jnp.exp(-jnp.sum(depth_values, axis=0))
    return (colour, transmit)


def body(volume, resampler, ramp_slope, ramp_pivot, tile_owner, tile_cell, depth_order, slab_rank):
    brick_count = volume.shape[0]
    brick_edge = volume.shape[1]
    sample_cols = resampler.shape[2]
    view_count = resampler.shape[0]
    tile_count = lax.axis_size("tile")
    capacity = max(2, 2 * view_count * brick_count // tile_count)
    edge_ids = jnp.arange(brick_edge)
    strict_lower = (edge_ids[None, :] < edge_ids[:, None]).astype(jnp.float32)
    prints = lax.map(
        lambda brick: render_brick(brick, resampler, strict_lower, ramp_slope, ramp_pivot), volume
    )
    slot_total = tile_count * capacity
    targets = tile_owner.reshape(-1)
    slot_index = bucket_slots(targets)
    flat_prints = prints.reshape(brick_count * view_count, 4, brick_edge, sample_cols)
    view_tags = jnp.tile(jnp.arange(view_count, dtype=jnp.int32), brick_count)
    label_values = jnp.stack(
        [jnp.ones_like(targets), view_tags, tile_cell.reshape(-1), depth_order.T.reshape(-1)],
        axis=1,
    )
    buffer = jnp.zeros((tile_count, capacity, 4, brick_edge, sample_cols), jnp.float32)
    buffer = buffer.at[targets, slot_index].set(flat_prints)
    slot_tags = (
        jnp.zeros((tile_count, capacity, 4), jnp.int32).at[targets, slot_index].set(label_values)
    )
    received, got_tags = (
        lax.all_to_all(buffer, "tile", split_axis=0, concat_axis=0, tiled=True),
        lax.all_to_all(slot_tags, "tile", split_axis=0, concat_axis=0, tiled=True),
    )
    received = received.reshape(slot_total, 4, brick_edge, sample_cols)
    got_tags = got_tags.reshape(slot_total, 4)
    slab_tile_piece = compose(
        received, got_tags[:, 0] == 1, got_tags[:, 1], got_tags[:, 2], got_tags[:, 3], view_count
    )
    row_bands = lax.all_to_all(
        slab_tile_piece[None], "depth", split_axis=3, concat_axis=0, tiled=True
    ).astype(jnp.float32)
    colour, transmit = blend_slabs(row_bands, slab_rank)
    return (colour[:, :, None], transmit[:, None])


def solution(mesh):
    in_specs = (
        P(("depth", "tile"), None, None, None),
        P(),
        P(),
        P(),
        P(("depth", "tile"), None),
        P(("depth", "tile"), None),
        P(None, ("depth", "tile")),
        P(),
    )
    out_specs = (P(None, None, "tile", "depth", None), P(None, "tile", "depth", None))
    return jax.shard_map(body, mesh=mesh, in_specs=in_specs, out_specs=out_specs, check_vma=False)
```

profile of v0, /device:TPU:0, one launch (start us, length us, event | category | flops | bytes accessed | tf_op | source)
XLA Modules:
  0.0 616.2 jit_solution(5227709136763322359)
XLA Ops:
  6.5 7.3 %all-to-all-start.1 = ((s32[8,8,4]{1,2,0:T(4,128)}), s32[8,8,4]{1,2,0:T(4,128)S(1)}, u32[]{:S(2)}, u32[]{:S(2)}) async-start(s32[8,8,4]{1,2,0:T(4,128)} %copy.85), calls=%async_computation.1 | async-start | bytes 32768 | tf_op jit(solution)/shard_map/all_to_all | solution.py:95
  13.9 362.4 %while.11 = (s32[]{:T(128)}, f32[16,2,4,64,128]{4,3,2,1,0:T(8,128)}, bf16[16,64,64,64]{3,2,1,0:T(8,128)(2,1)}, bf16[2,64,128]{2,1,0:T(8,128)(2,1)}, f32[3]{0:T(128)}, /*index=5*/f32[3]{0:T(128)}, s32[]{:T(128)}) while((s32[]{:T(128)}, f32[16,2,4,64,128]{4,3,2,1,0:T(8,128)}, bf16[16,64,64,64]{3,2,1,0:T(8,128)(2,1)}, ...), condition=%wide.region_6.7_spmd.clone, body=%wide.region_1.6_spmd.clone.sunk | while | flops 971120640 | bytes 34504896 | solution.py:76
  26.5 9.3 %multiply_reduce_fusion.5 = (f32[2,64,128]{2,1,0:T(8,128)S(1)}, f32[2,64,128]{2,1,0:T(8,128)S(1)}, f32[2,64,128]{2,1,0:T(8,128)S(1)}, f32[2,64,128]{2,1,0:T(8,128)S(1)}) fusion(f32[2,64,128,64]{2,3,1,0:T(8,128)S(1)} %fusion.81, f32[]{:T(128)} %bitcast.168, f32[]{:T(128)} %bitcast.169, f32[1,64,64,128]{3,2,1,0:T(8,128)S(1)} %convolution_bitcast_fusion.4, ...), kind=kLoop, calls=%fused_computation.11.clone.1 | loop fusion | flops 29294592 | bytes 8650776 | tf_op jit(solution)/shard_map/while/body/eval_jaxpr/reduce_sum | solution.py:25
  49.2 9.3 %multiply_reduce_fusion.5 = (f32[2,64,128]{2,1,0:T(8,128)S(1)}, f32[2,64,128]{2,1,0:T(8,128)S(1)}, f32[2,64,128]{2,1,0:T(8,128)S(1)}, f32[2,64,128]{2,1,0:T(8,128)S(1)}) fusion(f32[2,64,128,64]{2,3,1,0:T(8,128)S(1)} %fusion.81, f32[]{:T(128)} %bitcast.168, f32[]{:T(128)} %bitcast.169, f32[1,64,64,128]{3,2,1,0:T(8,128)S(1)} %convolution_bitcast_fusion.4, ...), kind=kLoop, calls=%fused_computation.11.clone.1 | loop fusion | flops 29294592 | bytes 8650776 | tf_op jit(solution)/shard_map/while/body/eval_jaxpr/reduce_sum | solution.py:25
  71.8 9.3 %multiply_reduce_fusion.5 = (f32[2,64,128]{2,1,0:T(8,128)S(1)}, f32[2,64,128]{2,1,0:T(8,128)S(1)}, f32[2,64,128]{2,1,0:T(8,128)S(1)}, f32[2,64,128]{2,1,0:T(8,128)S(1)}) fusion(f32[2,64,128,64]{2,3,1,0:T(8,128)S(1)} %fusion.81, f32[]{:T(128)} %bitcast.168, f32[]{:T(128)} %bitcast.169, f32[1,64,64,128]{3,2,1,0:T(8,128)S(1)} %convolution_bitcast_fusion.4, ...), kind=kLoop, calls=%fused_computation.11.clone.1 | loop fusion | flops 29294592 | bytes 8650776 | tf_op jit(solution)/shard_map/while/body/eval_jaxpr/reduce_sum | solution.py:25
  94.5 9.3 %multiply_reduce_fusion.5 = (f32[2,64,128]{2,1,0:T(8,128)S(1)}, f32[2,64,128]{2,1,0:T(8,128)S(1)}, f32[2,64,128]{2,1,0:T(8,128)S(1)}, f32[2,64,128]{2,1,0:T(8,128)S(1)}) fusion(f32[2,64,128,64]{2,3,1,0:T(8,128)S(1)} %fusion.81, f32[]{:T(128)} %bitcast.168, f32[]{:T(128)} %bitcast.169, f32[1,64,64,128]{3,2,1,0:T(8,128)S(1)} %convolution_bitcast_fusion.4, ...), kind=kLoop, calls=%fused_computation.11.clone.1 | loop fusion | flops 29294592 | bytes 8650776 | tf_op jit(solution)/shard_map/while/body/eval_jaxpr/reduce_sum | solution.py:25
  117.2 9.3 %multiply_reduce_fusion.5 = (f32[2,64,128]{2,1,0:T(8,128)S(1)}, f32[2,64,128]{2,1,0:T(8,128)S(1)}, f32[2,64,128]{2,1,0:T(8,128)S(1)}, f32[2,64,128]{2,1,0:T(8,128)S(1)}) fusion(f32[2,64,128,64]{2,3,1,0:T(8,128)S(1)} %fusion.81, f32[]{:T(128)} %bitcast.168, f32[]{:T(128)} %bitcast.169, f32[1,64,64,128]{3,2,1,0:T(8,128)S(1)} %convolution_bitcast_fusion.4, ...), kind=kLoop, calls=%fused_computation.11.clone.1 | loop fusion | flops 29294592 | bytes 8650776 | tf_op jit(solution)/shard_map/while/body/eval_jaxpr/reduce_sum | solution.py:25
  139.8 9.3 %multiply_reduce_fusion.5 = (f32[2,64,128]{2,1,0:T(8,128)S(1)}, f32[2,64,128]{2,1,0:T(8,128)S(1)}, f32[2,64,128]{2,1,0:T(8,128)S(1)}, f32[2,64,128]{2,1,0:T(8,128)S(1)}) fusion(f32[2,64,128,64]{2,3,1,0:T(8,128)S(1)} %fusion.81, f32[]{:T(128)} %bitcast.168, f32[]{:T(128)} %bitcast.169, f32[1,64,64,128]{3,2,1,0:T(8,128)S(1)} %convolution_bitcast_fusion.4, ...), kind=kLoop, calls=%fused_computation.11.clone.1 | loop fusion | flops 29294592 | bytes 8650776 | tf_op jit(solution)/shard_map/while/body/eval_jaxpr/reduce_sum | solution.py:25
  155.8 6.6 %fusion.81 = f32[2,64,128,64]{2,3,1,0:T(8,128)S(1)} fusion(f32[2,64,64,128]{3,2,1,0:T(8,128)S(1)} %broadcast_multiply_fusion.2), kind=kOutput, calls=%fused_computation.7.clone.1 | convolution fusion | flops 805314560 | bytes 8388608 | tf_op jit(solution)/shard_map/while/body/eval_jaxpr/kj,vjrs->vkrs/dot_general | solution.py:20
  162.5 9.3 %multiply_reduce_fusion.5 = (f32[2,64,128]{2,1,0:T(8,128)S(1)}, f32[2,64,128]{2,1,0:T(8,128)S(1)}, f32[2,64,128]{2,1,0:T(8,128)S(1)}, f32[2,64,128]{2,1,0:T(8,128)S(1)}) fusion(f32[2,64,128,64]{2,3,1,0:T(8,128)S(1)} %fusion.81, f32[]{:T(128)} %bitcast.168, f32[]{:T(128)} %bitcast.169, f32[1,64,64,128]{3,2,1,0:T(8,128)S(1)} %convolution_bitcast_fusion.4, ...), kind=kLoop, calls=%fused_computation.11.clone.1 | loop fusion | flops 29294592 | bytes 8650776 | tf_op jit(solution)/shard_map/while/body/eval_jaxpr/reduce_sum | solution.py:25
  185.1 9.3 %multiply_reduce_fusion.5 = (f32[2,64,128]{2,1,0:T(8,128)S(1)}, f32[2,64,128]{2,1,0:T(8,128)S(1)}, f32[2,64,128]{2,1,0:T(8,128)S(1)}, f32[2,64,128]{2,1,0:T(8,128)S(1)}) fusion(f32[2,64,128,64]{2,3,1,0:T(8,128)S(1)} %fusion.81, f32[]{:T(128)} %bitcast.168, f32[]{:T(128)} %bitcast.169, f32[1,64,64,128]{3,2,1,0:T(8,128)S(1)} %convolution_bitcast_fusion.4, ...), kind=kLoop, calls=%fused_computation.11.clone.1 | loop fusion | flops 29294592 | bytes 8650776 | tf_op jit(solution)/shard_map/while/body/eval_jaxpr/reduce_sum | solution.py:25
  201.1 6.6 %fusion.81 = f32[2,64,128,64]{2,3,1,0:T(8,128)S(1)} fusion(f32[2,64,64,128]{3,2,1,0:T(8,128)S(1)} %broadcast_multiply_fusion.2), kind=kOutput, calls=%fused_computation.7.clone.1 | convolution fusion | flops 805314560 | bytes 8388608 | tf_op jit(solution)/shard_map/while/body/eval_jaxpr/kj,vjrs->vkrs/dot_general | solution.py:20
  207.7 9.3 %multiply_reduce_fusion.5 = (f32[2,64,128]{2,1,0:T(8,128)S(1)}, f32[2,64,128]{2,1,0:T(8,128)S(1)}, f32[2,64,128]{2,1,0:T(8,128)S(1)}, f32[2,64,128]{2,1,0:T(8,128)S(1)}) fusion(f32[2,64,128,64]{2,3,1,0:T(8,128)S(1)} %fusion.81, f32[]{:T(128)} %bitcast.168, f32[]{:T(128)} %bitcast.169, f32[1,64,64,128]{3,2,1,0:T(8,128)S(1)} %convolution_bitcast_fusion.4, ...), kind=kLoop, calls=%fused_computation.11.clone.1 | loop fusion | flops 29294592 | bytes 8650776 | tf_op jit(solution)/shard_map/while/body/eval_jaxpr/reduce_sum | solution.py:25
  230.4 9.3 %multiply_reduce_fusion.5 = (f32[2,64,128]{2,1,0:T(8,128)S(1)}, f32[2,64,128]{2,1,0:T(8,128)S(1)}, f32[2,64,128]{2,1,0:T(8,128)S(1)}, f32[2,64,128]{2,1,0:T(8,128)S(1)}) fusion(f32[2,64,128,64]{2,3,1,0:T(8,128)S(1)} %fusion.81, f32[]{:T(128)} %bitcast.168, f32[]{:T(128)} %bitcast.169, f32[1,64,64,128]{3,2,1,0:T(8,128)S(1)} %convolution_bitcast_fusion.4, ...), kind=kLoop, calls=%fused_computation.11.clone.1 | loop fusion | flops 29294592 | bytes 8650776 | tf_op jit(solution)/shard_map/while/body/eval_jaxpr/reduce_sum | solution.py:25
  253.0 9.3 %multiply_reduce_fusion.5 = (f32[2,64,128]{2,1,0:T(8,128)S(1)}, f32[2,64,128]{2,1,0:T(8,128)S(1)}, f32[2,64,128]{2,1,0:T(8,128)S(1)}, f32[2,64,128]{2,1,0:T(8,128)S(1)}) fusion(f32[2,64,128,64]{2,3,1,0:T(8,128)S(1)} %fusion.81, f32[]{:T(128)} %bitcast.168, f32[]{:T(128)} %bitcast.169, f32[1,64,64,128]{3,2,1,0:T(8,128)S(1)} %convolution_bitcast_fusion.4, ...), kind=kLoop, calls=%fused_computation.11.clone.1 | loop fusion | flops 29294592 | bytes 8650776 | tf_op jit(solution)/shard_map/while/body/eval_jaxpr/reduce_sum | solution.py:25
  275.7 9.3 %multiply_reduce_fusion.5 = (f32[2,64,128]{2,1,0:T(8,128)S(1)}, f32[2,64,128]{2,1,0:T(8,128)S(1)}, f32[2,64,128]{2,1,0:T(8,128)S(1)}, f32[2,64,128]{2,1,0:T(8,128)S(1)}) fusion(f32[2,64,128,64]{2,3,1,0:T(8,128)S(1)} %fusion.81, f32[]{:T(128)} %bitcast.168, f32[]{:T(128)} %bitcast.169, f32[1,64,64,128]{3,2,1,0:T(8,128)S(1)} %convolution_bitcast_fusion.4, ...), kind=kLoop, calls=%fused_computation.11.clone.1 | loop fusion | flops 29294592 | bytes 8650776 | tf_op jit(solution)/shard_map/while/body/eval_jaxpr/reduce_sum | solution.py:25
  298.3 9.3 %multiply_reduce_fusion.5 = (f32[2,64,128]{2,1,0:T(8,128)S(1)}, f32[2,64,128]{2,1,0:T(8,128)S(1)}, f32[2,64,128]{2,1,0:T(8,128)S(1)}, f32[2,64,128]{2,1,0:T(8,128)S(1)}) fusion(f32[2,64,128,64]{2,3,1,0:T(8,128)S(1)} %fusion.81, f32[]{:T(128)} %bitcast.168, f32[]{:T(128)} %bitcast.169, f32[1,64,64,128]{3,2,1,0:T(8,128)S(1)} %convolution_bitcast_fusion.4, ...), kind=kLoop, calls=%fused_computation.11.clone.1 | loop fusion | flops 29294592 | bytes 8650776 | tf_op jit(solution)/shard_map/while/body/eval_jaxpr/reduce_sum | solution.py:25
  321.0 9.3 %multiply_reduce_fusion.5 = (f32[2,64,128]{2,1,0:T(8,128)S(1)}, f32[2,64,128]{2,1,0:T(8,128)S(1)}, f32[2,64,128]{2,1,0:T(8,128)S(1)}, f32[2,64,128]{2,1,0:T(8,128)S(1)}) fusion(f32[2,64,128,64]{2,3,1,0:T(8,128)S(1)} %fusion.81, f32[]{:T(128)} %bitcast.168, f32[]{:T(128)} %bitcast.169, f32[1,64,64,128]{3,2,1,0:T(8,128)S(1)} %convolution_bitcast_fusion.4, ...), kind=kLoop, calls=%fused_computation.11.clone.1 | loop fusion | flops 29294592 | bytes 8650776 | tf_op jit(solution)/shard_map/while/body/eval_jaxpr/reduce_sum | solution.py:25
  343.6 9.3 %multiply_reduce_fusion.5 = (f32[2,64,128]{2,1,0:T(8,128)S(1)}, f32[2,64,128]{2,1,0:T(8,128)S(1)}, f32[2,64,128]{2,1,0:T(8,128)S(1)}, f32[2,64,128]{2,1,0:T(8,128)S(1)}) fusion(f32[2,64,128,64]{2,3,1,0:T(8,128)S(1)} %fusion.81, f32[]{:T(128)} %bitcast.168, f32[]{:T(128)} %bitcast.169, f32[1,64,64,128]{3,2,1,0:T(8,128)S(1)} %convolution_bitcast_fusion.4, ...), kind=kLoop, calls=%fused_computation.11.clone.1 | loop fusion | flops 29294592 | bytes 8650776 | tf_op jit(solution)/shard_map/while/body/eval_jaxpr/reduce_sum | solution.py:25
  366.3 9.3 %multiply_reduce_fusion.5 = (f32[2,64,128]{2,1,0:T(8,128)S(1)}, f32[2,64,128]{2,1,0:T(8,128)S(1)}, f32[2,64,128]{2,1,0:T(8,128)S(1)}, f32[2,64,128]{2,1,0:T(8,128)S(1)}) fusion(f32[2,64,128,64]{2,3,1,0:T(8,128)S(1)} %fusion.81, f32[]{:T(128)} %bitcast.168, f32[]{:T(128)} %bitcast.169, f32[1,64,64,128]{3,2,1,0:T(8,128)S(1)} %convolution_bitcast_fusion.4, ...), kind=kLoop, calls=%fused_computation.11.clone.1 | loop fusion | flops 29294592 | bytes 8650776 | tf_op jit(solution)/shard_map/while/body/eval_jaxpr/reduce_sum | solution.py:25
  380.5 8.6 %scatter_fusion = f32[8,8,4,64,128]{4,3,2,1,0:T(8,128)} fusion(f32[8,8,4,64,128]{4,3,2,1,0:T(8,128)} %broadcast_in_dim.12, s32[32]{0:T(128)S(1)} %fusion.59, f32[32,4,64,128]{3,2,1,0:T(8,128)} %bitcast.184), kind=kCustom, calls=%fused_computation | custom fusion | bytes 12583168 | tf_op jit(solution)/shard_map/scatter | solution.py:89
  395.4 182.4 %all-to-all-done = f32[8,8,4,64,128]{4,3,2,1,0:T(8,128)} async-done(((f32[8,8,4,64,128]{4,3,2,1,0:T(8,128)}), f32[8,8,4,64,128]{4,3,2,1,0:T(8,128)}, u32[]{:S(2)}, u32[]{:S(2)}) %all-to-all-start) | async-done | bytes 8388640 | tf_op jit(solution)/shard_map/all_to_all | solution.py:94
  577.8 8.2 %copy.131 = f32[8,8,4,64,128]{4,1,0,3,2:T(8,128)S(1)} copy(f32[8,8,4,64,128]{4,3,2,1,0:T(8,128)} %all-to-all-done) | data formatting | bytes 16777216 | tf_op jit(solution)/shard_map/all_to_all | solution.py:94
  594.8 17.0 %all_to_all.28 = bf16[1,2,4,512,128]{4,2,1,0,3:T(4,128)(2,1)S(1)} all-to-all(bf16[1,2,4,512,128]{4,2,1,0,3:T(4,128)(2,1)S(1)} %copy.92), channel_id=1, replica_groups=mesh['depth'=4,'tile'=8] {'depth'}, dimensions={3} | all-to-all | bytes 2097152 | tf_op jit(solution)/shard_map/all_to_all | solution.py:102
  (202 shorter events, 229.7 us)
Async XLA Ops:
  6.5 382.6 %all-to-all-start.1 = ((s32[8,8,4]{1,2,0:T(4,128)}), s32[8,8,4]{1,2,0:T(4,128)S(1)}, u32[]{:S(2)}, u32[]{:S(2)}) async-start(s32[8,8,4]{1,2,0:T(4,128)} %copy.85), calls=%async_computation.1 | async-start | bytes 32768 | tf_op jit(solution)/shard_map/all_to_all | solution.py:95
  13.9 4.4 copy-start
  36.5 4.4 copy-start
  59.2 4.4 copy-start
  81.8 4.4 copy-start
  104.5 4.4 copy-start
  127.2 4.4 copy-start
  149.8 4.4 copy-start
  172.5 4.4 copy-start
  195.1 4.4 copy-start
  217.7 4.4 copy-start
  240.4 4.4 copy-start
  263.1 4.4 copy-start
  285.7 4.4 copy-start
  308.3 4.4 copy-start
  331.0 4.4 copy-start
  353.6 4.4 copy-start
  389.2 188.6 %all-to-all-start = ((f32[8,8,4,64,128]{4,3,2,1,0:T(8,128)}), f32[8,8,4,64,128]{4,3,2,1,0:T(8,128)}, u32[]{:S(2)}, u32[]{:S(2)}) async-start(f32[8,8,4,64,128]{4,3,2,1,0:T(8,128)} %scatter_fusion), calls=%async_computation | async-start | bytes 16777216 | tf_op jit(solution)/shard_map/all_to_all | solution.py:94
  594.0 19.2 %copy-start.1 = (s32[2,4]{1,0:T(2,128)S(1)}, s32[2,4]{1,0:T(2,128)}, u32[]{:S(2)}) copy-start(s32[2,4]{1,0:T(2,128)} %param.17) | copy-start | bytes 100
where the time goes:
time: 619 us; the launch traced here: 616 us
  waiting for transfers between devices  182 us (29%)
  other arithmetic  177 us (29%)
  matrix products  125 us (20%)
  local copies, waits for them, and re-layouts  100 us (16%)
  blocking collectives  17 us (3%)
  starting transfers between devices  13.4 us (2%)
    all_to_all x1, waiting for transfers between devices, body(): lax.all_to_all(buffer, 'tile', split_axis=0, concat_axis=0, tiled=True)  182 us
    reduce_sum x16, other arithmetic, render_brick(): layers.append(jnp.sum(weight * tinted, axis=1))  148 us
    dot_general x16, matrix products, render_brick(): jnp.einsum('kj,vjrs->vkrs', strict_lower, optical, precision=TOP_PRECISION)  106 us
    squeeze x32, local copies, waits for them, and re-layouts, body(): lax.map(lambda brick: render_brick(brick, resampler, strict_lower, ramp_s...  46.6 us
    slice x16, local copies, waits for them, and re-layouts, render_brick(): ramp_slope[channel] * (samples - ramp_pivot[channel])  23.2 us
    all_to_all x1, blocking collectives, body(): lax.all_to_all(slab_tile_piece[None], 'depth', split_axis=3, concat_axis=...  17 us
    mul x16, other arithmetic, render_brick(): optical = samples * (EXTINCTION / samples.shape[1])  13.3 us
  transfers between devices with their start and end apart: 2, of which 1 were waited for; matrix products, arithmetic and copies ran while one was open for 61% of the time, Pallas kernels for 0%

commit v1 on v0

v1 whole, which is shorter than its diff:
```python
import functools

import jax
import jax.numpy as jnp
from jax import lax
from jax.experimental import pallas as pl
from jax.experimental.pallas import tpu as pltpu
from jax.sharding import PartitionSpec as P

LOG2E = 1.4426950408889634
GROUP = 8
CELLS = 8
AXES = ("depth", "tile")


def render_kernel(slope_ref, pivot_ref, vol_ref, res_ref, out_ref, even_ref, odd_ref, ramp_ref, acc_ref, seen_ref, tint_ref, print_ref, *, view):
    step = pl.program_id(0)
    bricks = pl.num_programs(0) - 1
    edge = vol_ref.shape[1]
    cols = res_ref.shape[1]
    blocks = edge // GROUP
    half = edge // 2
    rate = -LOG2E / edge

    def multiply(block, samp_ref):
        if view == 0:
            rows = vol_ref[0, pl.ds(block * GROUP, GROUP)].reshape(GROUP * edge, edge)
            made = jnp.dot(rows, res_ref[...], preferred_element_type=jnp.float32)
            samp_ref[pl.ds(block * GROUP * edge, GROUP * edge), :] = made
        else:
            for j in range(GROUP):
                made = lax.dot_general(
                    vol_ref[0, block * GROUP + j], res_ref[...], (((0,), (0,)), ((), ())),
                    preferred_element_type=jnp.float32)
                samp_ref[pl.ds(block * GROUP * (edge + 1) + j * (edge + 1), edge), :] = made

    def start():
        acc_ref[...] = jnp.zeros_like(acc_ref)
        seen_ref[...] = jnp.ones_like(seen_ref)
        tint_ref[...] = jnp.zeros_like(tint_ref)

    def ramps():
        for ch in range(3):
            gain = jnp.full((16, cols), 0.5 * slope_ref[ch], jnp.float32)
            offset = -gain * pivot_ref[ch]
            for place, value in ((0, gain), (1, offset)):
                debt = jnp.zeros_like(value)
                for j in range(GROUP):
                    want = value + debt
                    given = want.astype(jnp.bfloat16)
                    debt = want - given.astype(jnp.float32)
                    ramp_ref[j, ch, place] = given

    def march(block, samp_ref):
        for top in range(0, edge, half):
            acc = acc_ref[pl.ds(top, half), :]
            seen = seen_ref[pl.ds(top, half), :]
            part = [[] for _ in range(3)]
            for j in range(GROUP):
                if view == 0:
                    s = samp_ref[pl.ds((block * GROUP + j) * edge + top, half), :]
                else:
                    s = samp_ref[pl.ds(top * (edge + 1) + block * GROUP + j, half, stride=edge + 1), :]
                acc = acc + s
                left = jnp.exp2(acc * rate)
                w = (seen - left).astype(jnp.bfloat16)
                seen = left
                s16 = s.astype(jnp.bfloat16)
                for ch in range(3):
                    gain = jnp.concatenate([ramp_ref[j, ch, 0]] * (half // 16), axis=0)
                    offset = jnp.concatenate([ramp_ref[j, ch, 1]] * (half // 16), axis=0)
                    p = w * jnp.tanh(s16 * gain + offset)
                    n = j
                    while n % 2 == 1:
                        p = part[ch].pop() + p
                        n //= 2
                    part[ch].append(p)
            for ch in range(3):
                tint_ref[ch, pl.ds(top, half), :] += part[ch][0].astype(jnp.float32)
            acc_ref[pl.ds(top, half), :] = acc
            seen_ref[pl.ds(top, half), :] = seen

    def finish(brick):
        alpha = 1.0 - seen_ref[...]
        for ch in range(3):
            print_ref[pl.ds((ch * bricks + brick) * (edge + 1), edge), :] = 0.5 * (alpha + tint_ref[ch])
        print_ref[pl.ds((3 * bricks + brick) * (edge + 1), edge), :] = acc_ref[...] * (1.0 / edge)

    def loop(f):
        def it(block, carry):
            f(block)
            return carry
        lax.fori_loop(0, blocks, it, 0)

    @pl.when(step == 0)
    def _():
        ramps()
        loop(lambda block: multiply(block, even_ref))

    for parity, (own, other) in enumerate(((even_ref, odd_ref), (odd_ref, even_ref))):
        @pl.when((step > 0) & (step < bricks) & (lax.rem(step, 2) == parity))
        def _():
            start()

            def both(block):
                multiply(block, own)
                march(block, other)
            loop(both)
            finish(step - 1)

    last = odd_ref if last_slot_is_odd(out_ref) else even_ref

    @pl.when(step == bricks)
    def _():
        start()
        loop(lambda block: march(block, last))
        finish(step - 1)

        def swap(row, carry):
            out_ref[row] = print_ref[pl.ds(row, out_ref.shape[1], stride=edge + 1), :].astype(jnp.bfloat16)
            return carry
        lax.fori_loop(0, edge, swap, 0, unroll=4)


def last_slot_is_odd(out_ref):
    return (out_ref.shape[1] // 4 - 1) % 2 == 1


def render(volume, resampler, slope, pivot, view, first, count):
    edge, cols = volume.shape[1], resampler.shape[1]
    smem = pl.BlockSpec(memory_space=pltpu.SMEM)
    return pl.pallas_call(
        functools.partial(render_kernel, view=view),
        grid=(count + 1,),
        in_specs=[
            smem, smem,
            pl.BlockSpec((1, edge, edge, edge), lambda g: (first + jnp.minimum(g, count - 1), 0, 0, 0)),
            pl.BlockSpec((edge, cols), lambda g: (0, 0)),
        ],
        out_specs=pl.BlockSpec((edge, 4 * count, cols), lambda g: (0, 0, 0)),
        out_shape=jax.ShapeDtypeStruct((edge, 4 * count, cols), jnp.bfloat16),
        scratch_shapes=[
            pltpu.VMEM((edge * (edge + 1), cols), jnp.float32),
            pltpu.VMEM((edge * (edge + 1), cols), jnp.float32),
            pltpu.VMEM((GROUP, 3, 2, 16, cols), jnp.bfloat16),
            pltpu.VMEM((edge, cols), jnp.float32),
            pltpu.VMEM((edge, cols), jnp.float32),
            pltpu.VMEM((3, edge, cols), jnp.float32),
            pltpu.VMEM((4 * count * (edge + 1), cols), jnp.float32),
        ],
        name=f"render{view}",
    )(slope, pivot, volume, resampler)


def compose_kernel(row_ref, col_ref, *refs, base, halves):
    got, out_ref, feat_ref, sum_ref = refs[:halves], refs[halves], refs[halves + 1], refs[halves + 2]
    total, cols = feat_ref.shape[1:]
    places = sum_ref.shape[1]
    sources, _, slots, _ = got[0].shape
    bricks = slots // 4
    piece = sources * bricks
    for h in range(halves):
        for ch in range(4):
            part = got[h][:, 0, ch * bricks:(ch + 1) * bricks, :].astype(jnp.float32)
            feat_ref[ch, h * piece:(h + 1) * piece, :] = part.reshape(piece, cols).astype(jnp.bfloat16)
    sum_ref[...] = jnp.zeros_like(sum_ref)
    block = min(256, total)
    row = row_ref[...]
    start = lax.broadcasted_iota(jnp.int32, (places, block), 0) * base

    def it(i, carry):
        rows = pl.ds(i * block, block)
        code = col_ref[rows, 0:1]
        floor = col_ref[rows, 1:2]
        before = ((row >= floor) & (row < code)).astype(jnp.float32).astype(jnp.bfloat16)
        inner = jnp.dot(before, feat_ref[3], preferred_element_type=jnp.float32)
        light = jnp.exp(-inner)
        own = row_ref[:, rows]
        pick = ((own >= start) & (own < start + base)).astype(jnp.float32).astype(jnp.bfloat16)
        for ch in range(4):
            value = feat_ref[ch, rows, :]
            if ch < 3:
                value = (value.astype(jnp.float32) * light).astype(jnp.bfloat16)
            sum_ref[ch] += jnp.dot(pick, value, preferred_element_type=jnp.float32)
        return carry

    lax.fori_loop(0, total // block, it, 0)
    for ch in range(3):
        out_ref[:, 0, ch, :] = sum_ref[ch]
    out_ref[:, 0, 3, :] = jnp.exp(-sum_ref[3])


def compose(row, col, got, places, base):
    sources, bands, slots, cols = got[0].shape
    total = row.shape[1]
    halves = len(got)
    return pl.pallas_call(
        functools.partial(compose_kernel, base=base, halves=halves),
        grid=(bands,),
        in_specs=[
            pl.BlockSpec((1, total), lambda g: (0, 0)),
            pl.BlockSpec((total, 2), lambda g: (0, 0)),
        ] + [pl.BlockSpec((sources, 1, slots, cols), lambda g: (0, g, 0, 0))] * halves,
        out_specs=pl.BlockSpec((places, 1, 4, cols), lambda g: (0, g, 0, 0)),
        out_shape=jax.ShapeDtypeStruct((places, bands, 4, cols), jnp.float32),
        scratch_shapes=[
            pltpu.VMEM((4, total, cols), jnp.bfloat16),
            pltpu.VMEM((4, places, cols), jnp.float32),
        ],
        name="compose",
    )(row, col, *got)


def exchange(parts):
    return lax.all_to_all(parts, AXES, split_axis=0, concat_axis=0, tiled=True)


def body(volume, resampler, ramp_slope, ramp_pivot, tile_owner, tile_cell, depth_order, slab_rank):
    brick_count, edge = volume.shape[:2]
    views, _, cols = resampler.shape
    slabs, tiles = lax.axis_size("depth"), lax.axis_size("tile")
    devices = slabs * tiles
    cells_each = CELLS // slabs
    base = slabs * devices * brick_count
    places = devices * cells_each
    halves = 2
    chunk = brick_count // halves
    bands, groups = max(1, edge // devices), max(1, devices // edge)

    rank = lax.dynamic_slice_in_dim(slab_rank, lax.axis_index("depth"), 1, 1)
    key = rank * (devices * brick_count) + depth_order
    owner, cell = tile_owner.T, tile_cell.T
    place = ((cell // cells_each) * tiles + owner) * cells_each + cell % cells_each
    code = place * base + key
    codes = exchange(jnp.broadcast_to(code.reshape(1, -1), (devices, views * brick_count)))
    codes = codes.reshape(devices, views, halves, chunk).transpose(1, 2, 0, 3).reshape(views, -1)
    floors = (codes // base) * base

    finals = []
    for view in range(views):
        got = []
        for half in range(halves):
            prints = render(volume, resampler[view], ramp_slope, ramp_pivot, view, half * chunk, chunk)
            prints = prints.reshape(edge, 4 * chunk, groups, cols // groups).transpose(0, 2, 1, 3)
            got.append(exchange(prints.reshape(devices, bands, 4 * chunk, cols // groups)))
        col = jnp.stack([codes[view], floors[view]], axis=1)
        made = compose(codes[view][None], col, got, places, base)
        final = exchange(made.reshape(devices, cells_each * bands * 4, cols // groups))
        final = final.reshape(edge // bands, groups, cells_each, bands, 4, cols // groups)
        finals.append(final.transpose(4, 2, 0, 3, 1, 5).reshape(4, cells_each * edge, cols))
    final = jnp.stack(finals)
    return final[:, :3, None], final[:, 3:]


def solution(mesh):
    in_specs = (
        P(AXES, None, None, None),
        P(),
        P(),
        P(),
        P(AXES, None),
        P(AXES, None),
        P(None, AXES),
        P(),
    )
    out_specs = (P(None, None, "tile", "depth", None), P(None, "tile", "depth", None))
    return jax.shard_map(body, mesh=mesh, in_specs=in_specs, out_specs=out_specs, check_vma=False)
```

time: 619 us -> 153 us (0.25)
  other arithmetic: 177 us -> 3.13 us
  waiting for transfers between devices: 182 us -> 25 us
  matrix products: 125 us -> 0 us
  local copies, waits for them, and re-layouts: 100 us -> 6.02 us
  Pallas kernels: 0 us -> 81.5 us
  starting transfers between devices: 13.4 us -> 35.8 us
  blocking collectives: 17 us -> 0 us
    all_to_all x2 -> x7, waiting for transfers between devices: 182 us -> 25 us  [exchange(): return lax.all_to_all(parts, AXES, split_axis=0, concat_axis=0, tiled=True)]
    reduce_sum x19 -> x0, other arithmetic: 150 us -> none  [the longest x16 148 us: render_brick(): layers.append(jnp.sum(weight * tinted, axis=1))]
    dot_general x52 -> x0, matrix products: 125 us -> none  [the longest x16 106 us: render_brick(): jnp.einsum('kj,vjrs->vkrs', strict_lower, optical, precision=TOP_PRECISION)]
    pallas_call x0 -> x6, Pallas kernels: none -> 81.5 us  [the longest x4 73.3 us: render(): pl.pallas_call(functools.partial(render_kernel, view=view), grid=(count +...]
    squeeze x32 -> x1, local copies, waits for them, and re-layouts: 46.6 us -> 1.35 us  [body(): resampler[view]]
    slice x18 -> x5, local copies, waits for them, and re-layouts: 24.6 us -> 1.5 us  [body(): made = compose(codes[view][None], col, got, places, base)]
    all_to_all x2 -> x7, starting transfers between devices: 13.4 us -> 35.8 us  [exchange(): return lax.all_to_all(parts, AXES, split_axis=0, concat_axis=0, tiled=True)]
    all_to_all x1 -> x0, blocking collectives: 17 us -> none  [body(): lax.all_to_all(slab_tile_piece[None], 'depth', split_axis=3, concat_axis=...]
  transfers between devices with their start and end apart: 2 -> 7, of which waited for: 1 -> 3; matrix products, arithmetic and copies ran while one was open for 61% -> 3% of each run, Pallas kernels for 0% -> 53%
where the time goes in v1:
time: 153 us; the launch traced here: 152 us
  Pallas kernels  81.5 us (53%)
  starting transfers between devices  35.8 us (23%)
  waiting for transfers between devices  25 us (16%)
  local copies, waits for them, and re-layouts  6.02 us (4%)
  other arithmetic  3.13 us (2%)
    pallas_call x4, Pallas kernels, render(): pl.pallas_call(functools.partial(render_kernel, view=view), grid=(count +...  73.3 us
    all_to_all x7, starting transfers between devices, exchange(): return lax.all_to_all(parts, AXES, split_axis=0, concat_axis=0, tiled=True)  35.8 us
    all_to_all x7, waiting for transfers between devices, exchange(): return lax.all_to_all(parts, AXES, split_axis=0, concat_axis=0, tiled=True)  25 us
    pallas_call x2, Pallas kernels, compose(): pl.pallas_call(functools.partial(compose_kernel, base=base, halves=halves...  8.18 us
  transfers between devices with their start and end apart: 7, of which 3 were waited for; matrix products, arithmetic and copies ran while one was open for 3% of the time, Pallas kernels for 53%

profile of v1, /device:TPU:0, one launch (start us, length us, event | category | flops | bytes accessed | tf_op | source)
XLA Modules:
  0.0 152.3 jit_solution(7813975292406303929)
XLA Ops:
  0.6 0.9 multiply_reduce_fusion
  1.5 0.8 add_add_fusion
  3.0 7.3 %all-to-all-start = ((s32[32,1,32]{2,1,0:T(1,128)}), s32[32,1,32]{2,1,0:T(1,128)S(1)}, u32[]{:S(2)}, u32[]{:S(2)}) async-start(s32[32,1,32]{2,1,0:T(1,128)} %broadcast_in_dim.11), calls=%async_computation | async-start | bytes 32768 | tf_op jit(solution)/shard_map/all_to_all | solution.py:215
  10.3 1.4 slice_bitcast_fusion
  11.7 20.3 %render1.2 = bf16[64,32,128]{2,1,0:T(8,128)(2,1)} custom-call(f32[3]{0:T(128)} %slope_ref.7, f32[3]{0:T(128)} %pivot_ref.7, bf16[16,64,64,64]{3,2,1,0:T(8,128)(2,1)} %vol_ref.7, bf16[64,128]{1,0:T(8,128)(2,1)} %get-tuple-element.2.res_ref), custom_call_target="tpu_custom_call" | custom-call | tf_op jit(solution)/shard_map/render1/pallas_call | solution.py:132
  32.0 5.8 %all-to-all-start.4 = ((bf16[32,2,32,128]{3,2,1,0:T(8,128)(2,1)}), bf16[32,2,32,128]{3,2,1,0:T(8,128)(2,1)S(1)}, u32[]{:S(2)}, u32[]{:S(2)}) async-start(bf16[32,2,32,128]{3,2,1,0:T(8,128)(2,1)} %bitcast.67), calls=%async_computation.4 | async-start | bytes 1048576 | tf_op jit(solution)/shard_map/all_to_all | solution.py:215
  37.8 20.3 %render1.3 = bf16[64,32,128]{2,1,0:T(8,128)(2,1)} custom-call(f32[3]{0:T(128)} %slope_ref.7, f32[3]{0:T(128)} %pivot_ref.7, bf16[16,64,64,64]{3,2,1,0:T(8,128)(2,1)} %vol_ref.7, bf16[64,128]{1,0:T(8,128)(2,1)} %get-tuple-element.2.res_ref), custom_call_target="tpu_custom_call" | custom-call | tf_op jit(solution)/shard_map/render1/pallas_call | solution.py:132
  58.2 5.8 %all-to-all-start.5 = ((bf16[32,2,32,128]{3,2,1,0:T(8,128)(2,1)}), bf16[32,2,32,128]{3,2,1,0:T(8,128)(2,1)S(1)}, u32[]{:S(2)}, u32[]{:S(2)}) async-start(bf16[32,2,32,128]{3,2,1,0:T(8,128)(2,1)} %bitcast.66), calls=%async_computation.5 | async-start | bytes 1048576 | tf_op jit(solution)/shard_map/all_to_all | solution.py:215
  64.0 16.3 %render0.2 = bf16[64,32,128]{2,1,0:T(8,128)(2,1)} custom-call(f32[3]{0:T(128)} %slope_ref.7, f32[3]{0:T(128)} %pivot_ref.7, bf16[16,64,64,64]{3,2,1,0:T(8,128)(2,1)} %vol_ref.7, bf16[64,128]{1,0:T(8,128)(2,1)} %get-tuple-element.3.res_ref), custom_call_target="tpu_custom_call" | custom-call | tf_op jit(solution)/shard_map/render0/pallas_call | solution.py:132
  80.3 5.8 %all-to-all-start.1 = ((bf16[32,2,32,128]{3,2,1,0:T(8,128)(2,1)}), bf16[32,2,32,128]{3,2,1,0:T(8,128)(2,1)S(1)}, u32[]{:S(2)}, u32[]{:S(2)}) async-start(bf16[32,2,32,128]{3,2,1,0:T(8,128)(2,1)} %bitcast.68), calls=%async_computation.1 | async-start | bytes 1048576 | tf_op jit(solution)/shard_map/all_to_all | solution.py:215
  86.2 16.3 %render0.3 = bf16[64,32,128]{2,1,0:T(8,128)(2,1)} custom-call(f32[3]{0:T(128)} %slope_ref.7, f32[3]{0:T(128)} %pivot_ref.7, bf16[16,64,64,64]{3,2,1,0:T(8,128)(2,1)} %vol_ref.7, bf16[64,128]{1,0:T(8,128)(2,1)} %get-tuple-element.3.res_ref), custom_call_target="tpu_custom_call" | custom-call | tf_op jit(solution)/shard_map/render0/pallas_call | solution.py:132
  102.5 5.8 %all-to-all-start.2 = ((bf16[32,2,32,128]{3,2,1,0:T(8,128)(2,1)}), bf16[32,2,32,128]{3,2,1,0:T(8,128)(2,1)S(1)}, u32[]{:S(2)}, u32[]{:S(2)}) async-start(bf16[32,2,32,128]{3,2,1,0:T(8,128)(2,1)} %bitcast.65), calls=%async_computation.2 | async-start | bytes 1048576 | tf_op jit(solution)/shard_map/all_to_all | solution.py:215
  108.7 0.7 slice.39.row_ref
  109.5 0.9 copy.31.col_ref
  110.4 4.1 %compose.3 = f32[64,2,4,128]{3,2,1,0:T(4,128)} custom-call(s32[1,512]{1,0:T(1,128)} %slice.39.row_ref, s32[512,2]{1,0:T(8,128)} %copy.31.col_ref, bf16[32,2,32,128]{3,2,1,0:T(8,128)(2,1)} %copy-done.1, bf16[32,2,32,128]{3,2,1,0:T(8,128)(2,1)} %copy-done.3), custom_call_target="tpu_custom_call" | custom-call | tf_op jit(solution)/shard_map/compose/pallas_call | solution.py:197
  114.5 10.1 %all-to-all-done.2.refs_1_ = bf16[32,2,32,128]{3,2,1,0:T(8,128)(2,1)S(1)} async-done(((bf16[32,2,32,128]{3,2,1,0:T(8,128)(2,1)}), bf16[32,2,32,128]{3,2,1,0:T(8,128)(2,1)S(1)}, u32[]{:S(2)}, u32[]{:S(2)}) %all-to-all-start.2) | async-done | bytes 524320 | tf_op jit(solution)/shard_map/all_to_all | solution.py:215
  124.6 2.6 %all-to-all-start.6 = ((f32[32,16,128]{2,1,0:T(8,128)}), f32[32,16,128]{2,1,0:T(8,128)S(1)}, u32[]{:S(2)}, u32[]{:S(2)}) async-start(f32[32,16,128]{2,1,0:T(8,128)} %bitcast.71), calls=%async_computation.6 | async-start | bytes 524288 | tf_op jit(solution)/shard_map/all_to_all | solution.py:215
  127.4 0.7 slice.35.row_ref
  128.1 0.9 copy.27.col_ref
  128.9 4.1 %compose.2 = f32[64,2,4,128]{3,2,1,0:T(4,128)} custom-call(s32[1,512]{1,0:T(1,128)} %slice.35.row_ref, s32[512,2]{1,0:T(8,128)} %copy.27.col_ref, bf16[32,2,32,128]{3,2,1,0:T(8,128)(2,1)} %copy-done, bf16[32,2,32,128]{3,2,1,0:T(8,128)(2,1)} %copy-done.2), custom_call_target="tpu_custom_call" | custom-call | tf_op jit(solution)/shard_map/compose/pallas_call | solution.py:197
  133.0 4.6 %all-to-all-done.6 = f32[32,16,128]{2,1,0:T(8,128)S(1)} async-done(((f32[32,16,128]{2,1,0:T(8,128)}), f32[32,16,128]{2,1,0:T(8,128)S(1)}, u32[]{:S(2)}, u32[]{:S(2)}) %all-to-all-start.6) | async-done | bytes 262176 | tf_op jit(solution)/shard_map/all_to_all | solution.py:215
  137.6 2.6 %all-to-all-start.3 = ((f32[32,16,128]{2,1,0:T(8,128)}), f32[32,16,128]{2,1,0:T(8,128)S(1)}, u32[]{:S(2)}, u32[]{:S(2)}) async-start(f32[32,16,128]{2,1,0:T(8,128)} %bitcast.72), calls=%async_computation.3 | async-start | bytes 524288 | tf_op jit(solution)/shard_map/all_to_all | solution.py:215
  140.4 10.3 %all-to-all-done.3 = f32[32,16,128]{2,1,0:T(8,128)S(1)} async-done(((f32[32,16,128]{2,1,0:T(8,128)}), f32[32,16,128]{2,1,0:T(8,128)S(1)}, u32[]{:S(2)}, u32[]{:S(2)}) %all-to-all-start.3) | async-done | bytes 262176 | tf_op jit(solution)/shard_map/all_to_all | solution.py:215
  151.5 0.8 fusion.1
  (29 shorter events, 2.3 us)
Async XLA Ops:
  3.0 29.0 %all-to-all-start = ((s32[32,1,32]{2,1,0:T(1,128)}), s32[32,1,32]{2,1,0:T(1,128)S(1)}, u32[]{:S(2)}, u32[]{:S(2)}) async-start(s32[32,1,32]{2,1,0:T(1,128)} %broadcast_in_dim.11), calls=%async_computation | async-start | bytes 32768 | tf_op jit(solution)/shard_map/all_to_all | solution.py:215
  32.0 26.2 %all-to-all-start.4 = ((bf16[32,2,32,128]{3,2,1,0:T(8,128)(2,1)}), bf16[32,2,32,128]{3,2,1,0:T(8,128)(2,1)S(1)}, u32[]{:S(2)}, u32[]{:S(2)}) async-start(bf16[32,2,32,128]{3,2,1,0:T(8,128)(2,1)} %bitcast.67), calls=%async_computation.4 | async-start | bytes 1048576 | tf_op jit(solution)/shard_map/all_to_all | solution.py:215
  58.2 44.3 %copy-start.1 = (bf16[32,2,32,128]{3,2,1,0:T(8,128)(2,1)}, bf16[32,2,32,128]{3,2,1,0:T(8,128)(2,1)S(1)}, u32[]{:S(2)}) copy-start(bf16[32,2,32,128]{3,2,1,0:T(8,128)(2,1)S(1)} %all-to-all-done.4.refs_0_) | copy-start | bytes 1572868
  58.2 22.1 %all-to-all-start.5 = ((bf16[32,2,32,128]{3,2,1,0:T(8,128)(2,1)}), bf16[32,2,32,128]{3,2,1,0:T(8,128)(2,1)S(1)}, u32[]{:S(2)}, u32[]{:S(2)}) async-start(bf16[32,2,32,128]{3,2,1,0:T(8,128)(2,1)} %bitcast.66), calls=%async_computation.5 | async-start | bytes 1048576 | tf_op jit(solution)/shard_map/all_to_all | solution.py:215
  80.3 30.1 %copy-start.3 = (bf16[32,2,32,128]{3,2,1,0:T(8,128)(2,1)}, bf16[32,2,32,128]{3,2,1,0:T(8,128)(2,1)S(1)}, u32[]{:S(2)}) copy-start(bf16[32,2,32,128]{3,2,1,0:T(8,128)(2,1)S(1)} %all-to-all-done.5.refs_1_) | copy-start | bytes 1572868
  80.3 22.2 %all-to-all-start.1 = ((bf16[32,2,32,128]{3,2,1,0:T(8,128)(2,1)}), bf16[32,2,32,128]{3,2,1,0:T(8,128)(2,1)S(1)}, u32[]{:S(2)}, u32[]{:S(2)}) async-start(bf16[32,2,32,128]{3,2,1,0:T(8,128)(2,1)} %bitcast.68), calls=%async_computation.1 | async-start | bytes 1048576 | tf_op jit(solution)/shard_map/all_to_all | solution.py:215
  102.5 26.4 %copy-start = (bf16[32,2,32,128]{3,2,1,0:T(8,128)(2,1)}, bf16[32,2,32,128]{3,2,1,0:T(8,128)(2,1)S(1)}, u32[]{:S(2)}) copy-start(bf16[32,2,32,128]{3,2,1,0:T(8,128)(2,1)S(1)} %all-to-all-done.1.refs_0_) | copy-start | bytes 1572868
  102.5 22.1 %all-to-all-start.2 = ((bf16[32,2,32,128]{3,2,1,0:T(8,128)(2,1)}), bf16[32,2,32,128]{3,2,1,0:T(8,128)(2,1)S(1)}, u32[]{:S(2)}, u32[]{:S(2)}) async-start(bf16[32,2,32,128]{3,2,1,0:T(8,128)(2,1)} %bitcast.65), calls=%async_computation.2 | async-start | bytes 1048576 | tf_op jit(solution)/shard_map/all_to_all | solution.py:215
  124.6 4.3 %copy-start.2 = (bf16[32,2,32,128]{3,2,1,0:T(8,128)(2,1)}, bf16[32,2,32,128]{3,2,1,0:T(8,128)(2,1)S(1)}, u32[]{:S(2)}) copy-start(bf16[32,2,32,128]{3,2,1,0:T(8,128)(2,1)S(1)} %all-to-all-done.2.refs_1_) | copy-start | bytes 1572868
  124.6 13.0 %all-to-all-start.6 = ((f32[32,16,128]{2,1,0:T(8,128)}), f32[32,16,128]{2,1,0:T(8,128)S(1)}, u32[]{:S(2)}, u32[]{:S(2)}) async-start(f32[32,16,128]{2,1,0:T(8,128)} %bitcast.71), calls=%async_computation.6 | async-start | bytes 524288 | tf_op jit(solution)/shard_map/all_to_all | solution.py:215
  137.6 13.0 %all-to-all-start.3 = ((f32[32,16,128]{2,1,0:T(8,128)}), f32[32,16,128]{2,1,0:T(8,128)S(1)}, u32[]{:S(2)}, u32[]{:S(2)}) async-start(f32[32,16,128]{2,1,0:T(8,128)} %bitcast.72), calls=%async_computation.3 | async-start | bytes 524288 | tf_op jit(solution)/shard_map/all_to_all | solution.py:215

commit v2 on v1

v2 whole, which is shorter than its diff:
```python
import functools

import jax
import jax.numpy as jnp
from jax import lax
from jax.experimental import pallas as pl
from jax.experimental.pallas import tpu as pltpu
from jax.sharding import PartitionSpec as P

LOG2E = 1.4426950408889634
GROUP = 16
STRIP = 16
CELLS = 8
TAGS = 8
AXES = ("depth", "tile")


def render_kernel(slope_ref, pivot_ref, code_ref, vol_ref, res_ref, out_ref, even_ref, odd_ref, ramp_ref, acc_ref, seen_ref, tint_ref, print_ref, *, view, count, tagged):
    step = pl.program_id(0)
    bricks = count
    edge = vol_ref.shape[1]
    cols = res_ref.shape[2]
    pitch = edge + 1
    blocks = edge // GROUP
    strip = STRIP
    rate = -LOG2E / edge

    def multiply(block, samp_ref):
        weights = res_ref[0]
        if view == 0:
            rows = vol_ref[0, pl.ds(block * GROUP, GROUP)].reshape(GROUP * edge, edge)
            made = jnp.dot(rows, weights, preferred_element_type=jnp.float32)
            samp_ref[pl.ds(block * GROUP * edge, GROUP * edge), :] = made
        else:
            for j in range(GROUP):
                made = lax.dot_general(
                    vol_ref[0, block * GROUP + j], weights, (((0,), (0,)), ((), ())),
                    preferred_element_type=jnp.float32)
                samp_ref[pl.ds(block * GROUP * pitch + j * pitch, edge), :] = made

    def start():
        acc_ref[...] = jnp.zeros_like(acc_ref)
        seen_ref[...] = jnp.ones_like(seen_ref)
        tint_ref[...] = jnp.zeros_like(tint_ref)

    def ramps():
        for ch in range(3):
            gain = jnp.full((16, cols), 0.5 * slope_ref[ch], jnp.float32)
            offset = -gain * pivot_ref[ch]
            for place, value in ((0, gain), (1, offset)):
                debt = jnp.zeros_like(value)
                for j in range(GROUP):
                    want = value + debt
                    given = want.astype(jnp.bfloat16)
                    debt = want - given.astype(jnp.float32)
                    ramp_ref[j, ch, place] = given

    def march(block, samp_ref):
        for top in range(0, edge, strip):
            acc = acc_ref[pl.ds(top, strip), :]
            seen = seen_ref[pl.ds(top, strip), :]
            part = [[] for _ in range(3)]
            for j in range(GROUP):
                if view == 0:
                    s = samp_ref[pl.ds((block * GROUP + j) * edge + top, strip), :]
                else:
                    s = samp_ref[pl.ds(top * pitch + block * GROUP + j, strip, stride=pitch), :]
                acc = acc + s
                left = jnp.exp2(acc * rate)
                w = (seen - left).astype(jnp.bfloat16)
                seen = left
                s16 = s.astype(jnp.bfloat16)
                for ch in range(3):
                    gain = jnp.concatenate([ramp_ref[j, ch, 0]] * (strip // 16), axis=0)
                    offset = jnp.concatenate([ramp_ref[j, ch, 1]] * (strip // 16), axis=0)
                    p = w * jnp.tanh(s16 * gain + offset)
                    n = j
                    while n % 2 == 1:
                        p = part[ch].pop() + p
                        n //= 2
                    part[ch].append(p)
            for ch in range(3):
                tint_ref[ch, pl.ds(top, strip), :] += part[ch][0].astype(jnp.float32)
            acc_ref[pl.ds(top, strip), :] = acc
            seen_ref[pl.ds(top, strip), :] = seen

    def finish(brick):
        alpha = 1.0 - seen_ref[...]
        for ch in range(3):
            print_ref[pl.ds((ch * bricks + brick) * pitch, edge), :] = 0.5 * (alpha + tint_ref[ch])
        print_ref[pl.ds((3 * bricks + brick) * pitch, edge), :] = acc_ref[...] * (1.0 / edge)

    def loop(f):
        def it(block, carry):
            f(block)
            return carry
        lax.fori_loop(0, blocks, it, 0)

    @pl.when(step == 0)
    def _():
        ramps()
        loop(lambda block: multiply(block, even_ref))

    for parity, (own, other) in enumerate(((even_ref, odd_ref), (odd_ref, even_ref))):
        @pl.when((step > 0) & (step < bricks) & (lax.rem(step, 2) == parity))
        def _():
            start()

            def both(block):
                multiply(block, own)
                march(block, other)
            loop(both)
            finish(step - 1)

    last = odd_ref if count % 2 == 0 else even_ref

    @pl.when(step == bricks)
    def _():
        start()
        loop(lambda block: march(block, last))
        finish(step - 1)

        if tagged:
            code = jnp.broadcast_to(code_ref[...], (TAGS, cols))
            digit = lax.broadcasted_iota(jnp.int32, (TAGS, cols), 0)
            tags = jnp.where(digit == 0, code & 255, jnp.where(digit == 1, (code >> 8) & 255, code >> 16)).astype(jnp.float32)

        def swap(row, carry):
            out_ref[row, :4 * bricks, :] = print_ref[pl.ds(row, 4 * bricks, stride=pitch), :].astype(jnp.bfloat16)
            if tagged:
                out_ref[row, 4 * bricks:, :] = tags.astype(jnp.bfloat16)
            return carry
        lax.fori_loop(0, edge, swap, 0, unroll=4)


def render(volume, resampler, slope, pivot, code, view, first, count, tagged):
    edge, cols = volume.shape[1], resampler.shape[2]
    pitch = edge + 1
    slots = 4 * count + (TAGS if tagged else 0)
    smem = pl.BlockSpec(memory_space=pltpu.SMEM)
    return pl.pallas_call(
        functools.partial(render_kernel, view=view, count=count, tagged=tagged),
        grid=(count + 1,),
        in_specs=[
            smem,
            smem,
            pl.BlockSpec((1, cols), lambda g: (0, 0)),
            pl.BlockSpec((1, edge, edge, edge), lambda g: (first + jnp.minimum(g, count - 1), 0, 0, 0)),
            pl.BlockSpec((1, edge, cols), lambda g: (view, 0, 0)),
        ],
        out_specs=pl.BlockSpec((edge, slots, cols), lambda g: (0, 0, 0)),
        out_shape=jax.ShapeDtypeStruct((edge, slots, cols), jnp.bfloat16),
        scratch_shapes=[
            pltpu.VMEM((edge * pitch, cols), jnp.float32),
            pltpu.VMEM((edge * pitch, cols), jnp.float32),
            pltpu.VMEM((GROUP, 3, 2, 16, cols), jnp.bfloat16),
            pltpu.VMEM((edge, cols), jnp.float32),
            pltpu.VMEM((edge, cols), jnp.float32),
            pltpu.VMEM((3, edge, cols), jnp.float32),
            pltpu.VMEM((4 * count * pitch, cols), jnp.float32),
        ],
        name=f"render{view}",
    )(slope, pivot, code, volume, resampler)


def compose_kernel(row_ref, col_ref, got_ref, *refs, base, count):
    out_ref, feat_ref, sum_ref = refs[-3:]
    total, cols = feat_ref.shape[1:]
    places = sum_ref.shape[1]
    for ch in range(4):
        part = got_ref[:, 0, ch * count:(ch + 1) * count, :].astype(jnp.float32)
        feat_ref[ch] = part.reshape(total, cols).astype(jnp.bfloat16)
    sum_ref[...] = jnp.zeros_like(sum_ref)
    block = min(256, total)
    row = row_ref[...]
    start = lax.broadcasted_iota(jnp.int32, (places, block), 0) * base

    def it(i, carry):
        rows = pl.ds(i * block, block)
        code = col_ref[rows, 0:1]
        floor = col_ref[rows, 1:2]
        before = ((row >= floor) & (row < code)).astype(jnp.float32).astype(jnp.bfloat16)
        inner = jnp.dot(before, feat_ref[3], preferred_element_type=jnp.float32)
        light = jnp.exp(-inner)
        own = row_ref[:, rows]
        pick = ((own >= start) & (own < start + base)).astype(jnp.float32).astype(jnp.bfloat16)
        for ch in range(4):
            value = feat_ref[ch, rows, :]
            if ch < 3:
                value = (value.astype(jnp.float32) * light).astype(jnp.bfloat16)
            sum_ref[ch] += jnp.dot(pick, value, preferred_element_type=jnp.float32)
        return carry

    lax.fori_loop(0, total // block, it, 0)
    for ch in range(3):
        out_ref[:, 0, 0, ch, :] = sum_ref[ch]
    out_ref[:, 0, 0, 3, :] = jnp.exp(-sum_ref[3])


def compose(row, col, got, made, view, views, count, places, base):
    sources, bands, slots, cols = got.shape
    total = row.shape[1]
    more = [] if made is None else [made]
    return pl.pallas_call(
        functools.partial(compose_kernel, base=base, count=count),
        grid=(bands,),
        in_specs=[
            pl.BlockSpec((1, total), lambda g: (0, 0)),
            pl.BlockSpec((total, 2), lambda g: (0, 0)),
            pl.BlockSpec((sources, 1, slots, cols), lambda g: (0, g, 0, 0)),
        ] + [pl.BlockSpec(memory_space=pl.ANY)] * len(more),
        out_specs=pl.BlockSpec((places, 1, 1, 4, cols), lambda g: (0, view, g, 0, 0)),
        out_shape=jax.ShapeDtypeStruct((places, views, bands, 4, cols), jnp.float32),
        scratch_shapes=[
            pltpu.VMEM((4, total, cols), jnp.bfloat16),
            pltpu.VMEM((4, places, cols), jnp.float32),
        ],
        input_output_aliases={3: 0} if more else {},
        name="compose",
    )(row, col, got, *more)


def exchange(parts):
    return lax.all_to_all(parts, AXES, split_axis=0, concat_axis=0, tiled=True)


def body(volume, resampler, ramp_slope, ramp_pivot, tile_owner, tile_cell, depth_order, slab_rank):
    count, edge = volume.shape[:2]
    views, _, cols = resampler.shape
    slabs, tiles = lax.axis_size("depth"), lax.axis_size("tile")
    devices = slabs * tiles
    cells_each = CELLS // slabs
    base = slabs * devices * count
    places = devices * cells_each
    bands, groups = max(1, edge // devices), max(1, devices // edge)
    width = cols // groups

    rank = lax.dynamic_slice_in_dim(slab_rank, lax.axis_index("depth"), 1, 1)
    key = rank * (devices * count) + depth_order
    owner, cell = tile_owner.T, tile_cell.T
    place = ((cell // cells_each) * tiles + owner) * cells_each + cell % cells_each
    code = (place * base + key).reshape(1, views * count)
    code = jnp.tile(code, (1, cols // (views * count)))

    order = list(range(views))[::-1]
    made, codes = None, None
    for view in order:
        tagged = view == order[0]
        prints = render(volume, resampler, ramp_slope, ramp_pivot, code, view, 0, count, tagged)
        prints = prints.reshape(edge, -1, groups, width).transpose(0, 2, 1, 3)
        got = exchange(prints.reshape(devices, bands, -1, width))
        if tagged:
            digits = got[:, 0, 4 * count:4 * count + 3, :views * count].astype(jnp.int32)
            codes = digits[:, 0] + digits[:, 1] * 256 + digits[:, 2] * 65536
            codes = codes.reshape(devices, views, count).transpose(1, 0, 2).reshape(views, -1)
            floors = (codes // base) * base
        col = jnp.stack([codes[view], floors[view]], axis=1)
        made = compose(codes[view][None], col, got, made, view, views, count, places, base)
    final = exchange(made.reshape(devices, cells_each * views * bands * 4, width))
    final = final.reshape(edge // bands, groups, cells_each, views, bands, 4, width)
    final = final.transpose(3, 5, 2, 0, 4, 1, 6).reshape(views, 4, cells_each * edge, cols)
    return final[:, :3, None], final[:, 3:]


def solution(mesh):
    in_specs = (
        P(AXES, None, None, None),
        P(),
        P(),
        P(),
        P(AXES, None),
        P(AXES, None),
        P(None, AXES),
        P(),
    )
    out_specs = (P(None, None, "tile", "depth", None), P(None, "tile", "depth", None))
    return jax.shard_map(body, mesh=mesh, in_specs=in_specs, out_specs=out_specs, check_vma=False)
```

time: 153 us -> 124 us (0.81)
  starting transfers between devices: 35.8 us -> 11.4 us
  Pallas kernels: 81.5 us -> 62.6 us
  blocking collectives: 0 us -> 18.8 us
  waiting for transfers between devices: 25 us -> 21.3 us
    all_to_all x7 -> x2, starting transfers between devices: 35.8 us -> 11.4 us  [exchange(): return lax.all_to_all(parts, AXES, split_axis=0, concat_axis=0, tiled=True)]
    pallas_call x6 -> x4, Pallas kernels: 81.5 us -> 62.6 us  [the longest x2 54.4 us: render(): pl.pallas_call(functools.partial(render_kernel, view=view, count=count, t...]
    all_to_all x0 -> x1, blocking collectives: none -> 18.8 us  [exchange(): return lax.all_to_all(parts, AXES, split_axis=0, concat_axis=0, tiled=True)]
    all_to_all x7 -> x2, waiting for transfers between devices: 25 us -> 21.3 us  [exchange(): return lax.all_to_all(parts, AXES, split_axis=0, concat_axis=0, tiled=True)]
  transfers between devices with their start and end apart: 7 -> 2, of which waited for: 3 -> 2; matrix products, arithmetic and copies ran while one was open for 3% -> 3% of each run, Pallas kernels for 53% -> 26%
where the time goes in v2:
time: 124 us
  Pallas kernels  62.6 us (50%)
  waiting for transfers between devices  21.3 us (17%)
  blocking collectives  18.8 us (15%)
  starting transfers between devices  11.4 us (9%)
  local copies, waits for them, and re-layouts  7 us (6%)
  other arithmetic  1.74 us (1%)
    pallas_call x2, Pallas kernels, render(): pl.pallas_call(functools.partial(render_kernel, view=view, count=count, t...  54.4 us
    all_to_all x2, waiting for transfers between devices, exchange(): return lax.all_to_all(parts, AXES, split_axis=0, concat_axis=0, tiled=True)  21.3 us
    all_to_all x1, blocking collectives, exchange(): return lax.all_to_all(parts, AXES, split_axis=0, concat_axis=0, tiled=True)  18.8 us
    all_to_all x2, starting transfers between devices, exchange(): return lax.all_to_all(parts, AXES, split_axis=0, concat_axis=0, tiled=True)  11.4 us
    pallas_call x2, Pallas kernels, compose(): pl.pallas_call(functools.partial(compose_kernel, base=base, count=count),...  8.16 us
  transfers between devices with their start and end apart: 2, of which 2 were waited for; matrix products, arithmetic and copies ran while one was open for 3% of the time, Pallas kernels for 26%

profile of v2, /device:TPU:0, one launch (start us, length us, event | category | flops | bytes accessed | tf_op | source)
XLA Modules:
  0.0 123.6 jit_solution(9355780327696144135)
XLA Ops:
  0.6 0.9 multiply_reduce_fusion
  1.5 0.8 add_add_fusion
  2.3 0.1 tile.10
  2.4 0.6 tile.12.code_ref
  3.0 25.8 %render1.1 = bf16[64,72,128]{2,1,0:T(8,128)(2,1)} custom-call(f32[3]{0:T(128)} %slope_ref.3, f32[3]{0:T(128)} %pivot_ref.3, s32[1,128]{1,0:T(1,128)} %tile.12.code_ref, bf16[16,64,64,64]{3,2,1,0:T(8,128)(2,1)} %vol_ref.3, bf16[2,64,128]{2,1,0:T(8,128)(2,1)} %res_ref.3), custom_call_target="tpu_custom_call" | custom-call | tf_op jit(solution)/shard_map/render1/pallas_call | solution.py:141
  28.8 7.3 %all-to-all-start = ((bf16[32,2,72,128]{3,2,1,0:T(8,128)(2,1)}), bf16[32,2,72,128]{3,2,1,0:T(8,128)(2,1)S(1)}, u32[]{:S(2)}, u32[]{:S(2)}) async-start(bf16[32,2,72,128]{3,2,1,0:T(8,128)(2,1)} %bitcast.47), calls=%async_computation | async-start | bytes 2359296 | tf_op jit(solution)/shard_map/all_to_all | solution.py:224
  36.1 28.6 %render0.1 = bf16[64,64,128]{2,1,0:T(8,128)(2,1)} custom-call(f32[3]{0:T(128)} %slope_ref.3, f32[3]{0:T(128)} %pivot_ref.3, s32[1,128]{1,0:T(1,128)} %tile.12.code_ref, bf16[16,64,64,64]{3,2,1,0:T(8,128)(2,1)} %vol_ref.3, bf16[2,64,128]{2,1,0:T(8,128)(2,1)} %res_ref.3), custom_call_target="tpu_custom_call" | custom-call | tf_op jit(solution)/shard_map/render0/pallas_call | solution.py:141
  64.7 1.7 %all-to-all-done.got_ref = bf16[32,2,72,128]{3,2,1,0:T(8,128)(2,1)S(1)} async-done(((bf16[32,2,72,128]{3,2,1,0:T(8,128)(2,1)}), bf16[32,2,72,128]{3,2,1,0:T(8,128)(2,1)S(1)}, u32[]{:S(2)}, u32[]{:S(2)}) %all-to-all-start) | async-done | bytes 1179680 | tf_op jit(solution)/shard_map/all_to_all | solution.py:224
  66.4 4.1 %all-to-all-start.1 = ((bf16[32,2,64,128]{3,2,1,0:T(8,128)(2,1)}), bf16[32,2,64,128]{3,2,1,0:T(8,128)(2,1)S(1)}, u32[]{:S(2)}, u32[]{:S(2)}) async-start(bf16[32,2,64,128]{3,2,1,0:T(8,128)(2,1)} %bitcast.48), calls=%async_computation.1 | async-start | bytes 2097152 | tf_op jit(solution)/shard_map/all_to_all | solution.py:224
  70.9 0.1 stack_squeeze.14
  71.0 0.7 slice.46.row_ref
  71.7 0.1 stack_squeeze.12
  71.8 0.7 slice.43.row_ref
  72.5 0.1 reshape.38
  72.6 0.9 copy.40.col_ref
  73.5 0.9 copy.41.col_ref
  74.3 4.1 %compose.2.refs_0_ = f32[64,2,2,4,128]{4,3,2,1,0:T(4,128)} custom-call(s32[1,512]{1,0:T(1,128)} %slice.46.row_ref, s32[512,2]{1,0:T(8,128)} %copy.40.col_ref, bf16[32,2,72,128]{3,2,1,0:T(8,128)(2,1)} %copy-done), custom_call_target="tpu_custom_call" | custom-call | tf_op jit(solution)/shard_map/compose/pallas_call | solution.py:204
  78.4 19.6 %all-to-all-done.1.got_ref = bf16[32,2,64,128]{3,2,1,0:T(8,128)(2,1)S(1)} async-done(((bf16[32,2,64,128]{3,2,1,0:T(8,128)(2,1)}), bf16[32,2,64,128]{3,2,1,0:T(8,128)(2,1)S(1)}, u32[]{:S(2)}, u32[]{:S(2)}) %all-to-all-start.1) | async-done | bytes 1048608 | tf_op jit(solution)/shard_map/all_to_all | solution.py:224
  98.0 1.0 copy-done.1
  99.0 4.1 %compose.3 = f32[64,2,2,4,128]{4,3,2,1,0:T(4,128)} custom-call(s32[1,512]{1,0:T(1,128)} %slice.43.row_ref, s32[512,2]{1,0:T(8,128)} %copy.41.col_ref, bf16[32,2,64,128]{3,2,1,0:T(8,128)(2,1)} %copy-done.1, f32[64,2,2,4,128]{4,3,2,1,0:T(4,128)} %compose.2.refs_0_), custom_call_target="tpu_custom_call", output_to_operand_aliasing={{}: (3, {})} | custom-call | tf_op jit(solution)/shard_map/compose/pallas_call | solution.py:204
  103.1 18.8 %all_to_all.15 = f32[32,32,128]{2,1,0:T(8,128)S(1)} all-to-all(f32[32,32,128]{2,1,0:T(8,128)} %bitcast.46), channel_id=1, replica_groups=mesh['depth'=4,'tile'=8] {'depth','tile'}, dimensions={0} | all-to-all | bytes 1048576 | tf_op jit(solution)/shard_map/all_to_all | solution.py:224
  121.9 0.3 copy.42
  122.2 0.8 slice_bitcast_fusion
  123.0 0.7 slice.59
  (16 shorter events, 0.4 us)
Async XLA Ops:
  28.8 37.6 %all-to-all-start = ((bf16[32,2,72,128]{3,2,1,0:T(8,128)(2,1)}), bf16[32,2,72,128]{3,2,1,0:T(8,128)(2,1)S(1)}, u32[]{:S(2)}, u32[]{:S(2)}) async-start(bf16[32,2,72,128]{3,2,1,0:T(8,128)(2,1)} %bitcast.47), calls=%async_computation | async-start | bytes 2359296 | tf_op jit(solution)/shard_map/all_to_all | solution.py:224
  66.4 4.4 %copy-start = (bf16[32,2,72,128]{3,2,1,0:T(8,128)(2,1)}, bf16[32,2,72,128]{3,2,1,0:T(8,128)(2,1)S(1)}, u32[]{:S(2)}) copy-start(bf16[32,2,72,128]{3,2,1,0:T(8,128)(2,1)S(1)} %all-to-all-done.got_ref) | copy-start | bytes 3538948
  66.4 31.6 %all-to-all-start.1 = ((bf16[32,2,64,128]{3,2,1,0:T(8,128)(2,1)}), bf16[32,2,64,128]{3,2,1,0:T(8,128)(2,1)S(1)}, u32[]{:S(2)}, u32[]{:S(2)}) async-start(bf16[32,2,64,128]{3,2,1,0:T(8,128)(2,1)} %bitcast.48), calls=%async_computation.1 | async-start | bytes 2097152 | tf_op jit(solution)/shard_map/all_to_all | solution.py:224
  98.0 1.0 copy-start.1

commit v3 on v2

--- a/solution.py
+++ b/solution.py
@@ -164,12 +164,14 @@
 
 
 def compose_kernel(row_ref, col_ref, got_ref, *refs, base, count):
-    out_ref, feat_ref, sum_ref = refs[-3:]
-    total, cols = feat_ref.shape[1:]
+    out_ref, feat_ref, sum_ref, pack_ref = refs[-4:]
+    total, lanes = feat_ref.shape[1:]
     places = sum_ref.shape[1]
-    for ch in range(4):
-        part = got_ref[:, 0, ch * count:(ch + 1) * count, :].astype(jnp.float32)
-        feat_ref[ch] = part.reshape(total, cols).astype(jnp.bfloat16)
+    bands, width = got_ref.shape[1], got_ref.shape[3]
+    for band in range(bands):
+        for ch in range(4):
+            part = got_ref[:, band, ch * count:(ch + 1) * count, :].astype(jnp.float32)
+            feat_ref[ch, :, band * width:(band + 1) * width] = part.reshape(total, width).astype(jnp.bfloat16)
     sum_ref[...] = jnp.zeros_like(sum_ref)
     block = min(256, total)
     row = row_ref[...]
@@ -192,28 +194,28 @@
         return carry
 
     lax.fori_loop(0, total // block, it, 0)
-    for ch in range(3):
-        out_ref[:, 0, 0, ch, :] = sum_ref[ch]
-    out_ref[:, 0, 0, 3, :] = jnp.exp(-sum_ref[3])
+    for band in range(bands):
+        for ch in range(4):
+            value = sum_ref[ch, :, band * width:(band + 1) * width]
+            pack_ref[:, band * 4 + ch, :] = value if ch < 3 else jnp.exp(-value)
+    out_ref[:, 0] = pack_ref[...].astype(jnp.bfloat16)
 
 
 def compose(row, col, got, made, view, views, count, places, base):
-    sources, bands, slots, cols = got.shape
+    sources, bands, slots, width = got.shape
     total = row.shape[1]
     more = [] if made is None else [made]
+    vmem = pl.BlockSpec(memory_space=pltpu.VMEM)
     return pl.pallas_call(
         functools.partial(compose_kernel, base=base, count=count),
-        grid=(bands,),
-        in_specs=[
-            pl.BlockSpec((1, total), lambda g: (0, 0)),
-            pl.BlockSpec((total, 2), lambda g: (0, 0)),
-            pl.BlockSpec((sources, 1, slots, cols), lambda g: (0, g, 0, 0)),
-        ] + [pl.BlockSpec(memory_space=pl.ANY)] * len(more),
-        out_specs=pl.BlockSpec((places, 1, 1, 4, cols), lambda g: (0, view, g, 0, 0)),
-        out_shape=jax.ShapeDtypeStruct((places, views, bands, 4, cols), jnp.float32),
+        grid=(1,),
+        in_specs=[vmem, vmem, vmem] + [pl.BlockSpec(memory_space=pl.ANY)] * len(more),
+        out_specs=pl.BlockSpec((places, 1, bands * 4, width), lambda g: (0, view, 0, 0)),
+        out_shape=jax.ShapeDtypeStruct((places, views, bands * 4, width), jnp.bfloat16),
         scratch_shapes=[
-            pltpu.VMEM((4, total, cols), jnp.bfloat16),
-            pltpu.VMEM((4, places, cols), jnp.float32),
+            pltpu.VMEM((4, total, bands * width), jnp.bfloat16),
+            pltpu.VMEM((4, places, bands * width), jnp.float32),
+            pltpu.VMEM((places, bands * 4, width), jnp.float32),
         ],
         input_output_aliases={3: 0} if more else {},
         name="compose",
@@ -256,9 +258,10 @@
             floors = (codes // base) * base
         col = jnp.stack([codes[view], floors[view]], axis=1)
         made = compose(codes[view][None], col, got, made, view, views, count, places, base)
-    final = exchange(made.reshape(devices, cells_each * views * bands * 4, width))
+    final = exchange(made.reshape(devices, cells_each * views, bands * 4, width))
     final = final.reshape(edge // bands, groups, cells_each, views, bands, 4, width)
     final = final.transpose(3, 5, 2, 0, 4, 1, 6).reshape(views, 4, cells_each * edge, cols)
+    final = final.astype(jnp.float32)
     return final[:, :3, None], final[:, 3:]
 
 

time: 124 us -> 118 us (0.952)
  blocking collectives: 18.8 us -> 13 us
    all_to_all x1, blocking collectives: 18.8 us -> 13 us  [exchange(): return lax.all_to_all(parts, AXES, split_axis=0, concat_axis=0, tiled=True)]
  transfers between devices with their start and end apart: 2 -> 2, of which waited for: 2 -> 2; matrix products, arithmetic and copies ran while one was open for 3% -> 3% of each run, Pallas kernels for 26% -> 27%
where the time goes in v3:
time: 118 us; the launch traced here: 117 us
  Pallas kernels  61.6 us (52%)
  waiting for transfers between devices  21.8 us (18%)
  blocking collectives  13 us (11%)
  starting transfers between devices  11.4 us (10%)
  local copies, waits for them, and re-layouts  7 us (6%)
  other arithmetic  1.74 us (1%)
    pallas_call x2, Pallas kernels, render(): pl.pallas_call(functools.partial(render_kernel, view=view, count=count, t...  54.4 us
    all_to_all x2, waiting for transfers between devices, exchange(): return lax.all_to_all(parts, AXES, split_axis=0, concat_axis=0, tiled=True)  21.8 us
    all_to_all x1, blocking collectives, exchange(): return lax.all_to_all(parts, AXES, split_axis=0, concat_axis=0, tiled=True)  13 us
    all_to_all x2, starting transfers between devices, exchange(): return lax.all_to_all(parts, AXES, split_axis=0, concat_axis=0, tiled=True)  11.4 us
    pallas_call x2, Pallas kernels, compose(): pl.pallas_call(functools.partial(compose_kernel, base=base, count=count),...  7.17 us
  transfers between devices with their start and end apart: 2, of which 2 were waited for; matrix products, arithmetic and copies ran while one was open for 3% of the time, Pallas kernels for 27%

profile of v3, /device:TPU:0, one launch (start us, length us, event | category | flops | bytes accessed | tf_op | source)
XLA Modules:
  0.0 117.3 jit_solution(7289583785013903384)
XLA Ops:
  0.6 0.9 multiply_reduce_fusion
  1.5 0.8 add_add_fusion
  2.3 0.1 tile.10
  2.4 0.6 tile.12.code_ref
  3.0 25.8 %render1.1 = bf16[64,72,128]{2,1,0:T(8,128)(2,1)} custom-call(f32[3]{0:T(128)} %slope_ref.3, f32[3]{0:T(128)} %pivot_ref.3, s32[1,128]{1,0:T(1,128)} %tile.12.code_ref, bf16[16,64,64,64]{3,2,1,0:T(8,128)(2,1)} %vol_ref.3, bf16[2,64,128]{2,1,0:T(8,128)(2,1)} %res_ref.3), custom_call_target="tpu_custom_call" | custom-call | tf_op jit(solution)/shard_map/render1/pallas_call | solution.py:141
  28.8 7.3 %all-to-all-start = ((bf16[32,2,72,128]{3,2,1,0:T(8,128)(2,1)}), bf16[32,2,72,128]{3,2,1,0:T(8,128)(2,1)S(1)}, u32[]{:S(2)}, u32[]{:S(2)}) async-start(bf16[32,2,72,128]{3,2,1,0:T(8,128)(2,1)} %bitcast.49), calls=%async_computation | async-start | bytes 2359296 | tf_op jit(solution)/shard_map/all_to_all | solution.py:226
  36.1 28.6 %render0.1 = bf16[64,64,128]{2,1,0:T(8,128)(2,1)} custom-call(f32[3]{0:T(128)} %slope_ref.3, f32[3]{0:T(128)} %pivot_ref.3, s32[1,128]{1,0:T(1,128)} %tile.12.code_ref, bf16[16,64,64,64]{3,2,1,0:T(8,128)(2,1)} %vol_ref.3, bf16[2,64,128]{2,1,0:T(8,128)(2,1)} %res_ref.3), custom_call_target="tpu_custom_call" | custom-call | tf_op jit(solution)/shard_map/render0/pallas_call | solution.py:141
  64.7 1.7 %all-to-all-done.got_ref = bf16[32,2,72,128]{3,2,1,0:T(8,128)(2,1)S(1)} async-done(((bf16[32,2,72,128]{3,2,1,0:T(8,128)(2,1)}), bf16[32,2,72,128]{3,2,1,0:T(8,128)(2,1)S(1)}, u32[]{:S(2)}, u32[]{:S(2)}) %all-to-all-start) | async-done | bytes 1179680 | tf_op jit(solution)/shard_map/all_to_all | solution.py:226
  66.4 4.1 %all-to-all-start.1 = ((bf16[32,2,64,128]{3,2,1,0:T(8,128)(2,1)}), bf16[32,2,64,128]{3,2,1,0:T(8,128)(2,1)S(1)}, u32[]{:S(2)}, u32[]{:S(2)}) async-start(bf16[32,2,64,128]{3,2,1,0:T(8,128)(2,1)} %bitcast.50), calls=%async_computation.1 | async-start | bytes 2097152 | tf_op jit(solution)/shard_map/all_to_all | solution.py:226
  70.9 0.1 stack_squeeze.14
  71.0 0.7 slice.46.row_ref
  71.7 0.1 stack_squeeze.12
  71.8 0.7 slice.43.row_ref
  72.5 0.1 reshape.38
  72.6 0.9 copy.40.col_ref
  73.5 0.9 copy.41.col_ref
  74.3 3.6 %compose.2.refs_0_ = bf16[64,2,8,128]{3,2,1,0:T(8,128)(2,1)} custom-call(s32[1,512]{1,0:T(1,128)} %slice.46.row_ref, s32[512,2]{1,0:T(8,128)} %copy.40.col_ref, bf16[32,2,72,128]{3,2,1,0:T(8,128)(2,1)} %copy-done), custom_call_target="tpu_custom_call" | custom-call | tf_op jit(solution)/shard_map/compose/pallas_call | solution.py:209
  77.9 20.1 %all-to-all-done.1.got_ref = bf16[32,2,64,128]{3,2,1,0:T(8,128)(2,1)S(1)} async-done(((bf16[32,2,64,128]{3,2,1,0:T(8,128)(2,1)}), bf16[32,2,64,128]{3,2,1,0:T(8,128)(2,1)S(1)}, u32[]{:S(2)}, u32[]{:S(2)}) %all-to-all-start.1) | async-done | bytes 1048608 | tf_op jit(solution)/shard_map/all_to_all | solution.py:226
  98.0 1.0 copy-done.1
  99.0 3.6 %compose.3 = bf16[64,2,8,128]{3,2,1,0:T(8,128)(2,1)} custom-call(s32[1,512]{1,0:T(1,128)} %slice.43.row_ref, s32[512,2]{1,0:T(8,128)} %copy.41.col_ref, bf16[32,2,64,128]{3,2,1,0:T(8,128)(2,1)} %copy-done.1, bf16[64,2,8,128]{3,2,1,0:T(8,128)(2,1)} %compose.2.refs_0_), custom_call_target="tpu_custom_call", output_to_operand_aliasing={{}: (3, {})} | custom-call | tf_op jit(solution)/shard_map/compose/pallas_call | solution.py:209
  102.6 13.0 %all_to_all.15 = bf16[32,4,8,128]{3,2,1,0:T(8,128)(2,1)S(1)} all-to-all(bf16[32,4,8,128]{3,2,1,0:T(8,128)(2,1)} %bitcast.51), channel_id=1, replica_groups=mesh['depth'=4,'tile'=8] {'depth','tile'}, dimensions={0} | all-to-all | bytes 524288 | tf_op jit(solution)/shard_map/all_to_all | solution.py:226
  115.6 0.3 copy.42
  115.9 0.8 slice_bitcast_fusion
  116.7 0.7 slice.59
  (16 shorter events, 0.4 us)
Async XLA Ops:
  28.8 37.6 %all-to-all-start = ((bf16[32,2,72,128]{3,2,1,0:T(8,128)(2,1)}), bf16[32,2,72,128]{3,2,1,0:T(8,128)(2,1)S(1)}, u32[]{:S(2)}, u32[]{:S(2)}) async-start(bf16[32,2,72,128]{3,2,1,0:T(8,128)(2,1)} %bitcast.49), calls=%async_computation | async-start | bytes 2359296 | tf_op jit(solution)/shard_map/all_to_all | solution.py:226
  66.4 4.4 %copy-start = (bf16[32,2,72,128]{3,2,1,0:T(8,128)(2,1)}, bf16[32,2,72,128]{3,2,1,0:T(8,128)(2,1)S(1)}, u32[]{:S(2)}) copy-start(bf16[32,2,72,128]{3,2,1,0:T(8,128)(2,1)S(1)} %all-to-all-done.got_ref) | copy-start | bytes 3538948
  66.4 31.6 %all-to-all-start.1 = ((bf16[32,2,64,128]{3,2,1,0:T(8,128)(2,1)}), bf16[32,2,64,128]{3,2,1,0:T(8,128)(2,1)S(1)}, u32[]{:S(2)}, u32[]{:S(2)}) async-start(bf16[32,2,64,128]{3,2,1,0:T(8,128)(2,1)} %bitcast.50), calls=%async_computation.1 | async-start | bytes 2097152 | tf_op jit(solution)/shard_map/all_to_all | solution.py:226
  98.0 1.0 copy-start.1

commit v4 on v3

--- a/solution.py
+++ b/solution.py
@@ -197,8 +197,8 @@
     for band in range(bands):
         for ch in range(4):
             value = sum_ref[ch, :, band * width:(band + 1) * width]
-            pack_ref[:, band * 4 + ch, :] = value if ch < 3 else jnp.exp(-value)
-    out_ref[:, 0] = pack_ref[...].astype(jnp.bfloat16)
+            pack_ref[:, band * 4 + ch, :] = value if ch < 3 else jnp.exp(-0.5 * value)
+    out_ref[:, 0] = pack_ref[...].astype(out_ref.dtype)
 
 
 def compose(row, col, got, made, view, views, count, places, base):
@@ -211,7 +211,7 @@
         grid=(1,),
         in_specs=[vmem, vmem, vmem] + [pl.BlockSpec(memory_space=pl.ANY)] * len(more),
         out_specs=pl.BlockSpec((places, 1, bands * 4, width), lambda g: (0, view, 0, 0)),
-        out_shape=jax.ShapeDtypeStruct((places, views, bands * 4, width), jnp.bfloat16),
+        out_shape=jax.ShapeDtypeStruct((places, views, bands * 4, width), jnp.float32),
         scratch_shapes=[
             pltpu.VMEM((4, total, bands * width), jnp.bfloat16),
             pltpu.VMEM((4, places, bands * width), jnp.float32),
@@ -258,11 +258,11 @@
             floors = (codes // base) * base
         col = jnp.stack([codes[view], floors[view]], axis=1)
         made = compose(codes[view][None], col, got, made, view, views, count, places, base)
-    final = exchange(made.reshape(devices, cells_each * views, bands * 4, width))
+    final = exchange(made.astype(jnp.float16).reshape(devices, cells_each * views, bands * 4, width))
     final = final.reshape(edge // bands, groups, cells_each, views, bands, 4, width)
     final = final.transpose(3, 5, 2, 0, 4, 1, 6).reshape(views, 4, cells_each * edge, cols)
     final = final.astype(jnp.float32)
-    return final[:, :3, None], final[:, 3:]
+    return final[:, :3, None], jnp.square(final[:, 3:])
 
 
 def solution(mesh):

time: 118 us -> 119 us (level)
  other arithmetic: 1.74 us -> 3.54 us
where the time goes in v4:
time: 119 us; the launch traced here: 118 us
  Pallas kernels  61.7 us (52%)
  waiting for transfers between devices  21.7 us (18%)
  blocking collectives  12.6 us (11%)
  starting transfers between devices  11.4 us (10%)
  local copies, waits for them, and re-layouts  6.34 us (5%)
  other arithmetic  3.54 us (3%)
    pallas_call x2, Pallas kernels, render(): pl.pallas_call(functools.partial(render_kernel, view=view, count=count, t...  54.4 us
    all_to_all x2, waiting for transfers between devices, exchange(): return lax.all_to_all(parts, AXES, split_axis=0, concat_axis=0, tiled=True)  21.7 us
    all_to_all x1, blocking collectives, exchange(): return lax.all_to_all(parts, AXES, split_axis=0, concat_axis=0, tiled=True)  12.6 us
    all_to_all x2, starting transfers between devices, exchange(): return lax.all_to_all(parts, AXES, split_axis=0, concat_axis=0, tiled=True)  11.4 us
    pallas_call x2, Pallas kernels, compose(): pl.pallas_call(functools.partial(compose_kernel, base=base, count=count),...  7.32 us
  transfers between devices with their start and end apart: 2, of which 2 were waited for; matrix products, arithmetic and copies ran while one was open for 3% of the time, Pallas kernels for 27%

profile of v4, /device:TPU:0, one launch (start us, length us, event | category | flops | bytes accessed | tf_op | source)
XLA Modules:
  0.0 118.1 jit_solution(1788077634672022297)
XLA Ops:
  0.6 0.9 multiply_reduce_fusion
  1.5 0.8 add_add_fusion
  2.3 0.1 tile.10
  2.4 0.6 tile.12.code_ref
  3.0 25.8 %render1.1 = bf16[64,72,128]{2,1,0:T(8,128)(2,1)} custom-call(f32[3]{0:T(128)} %slope_ref.3, f32[3]{0:T(128)} %pivot_ref.3, s32[1,128]{1,0:T(1,128)} %tile.12.code_ref, bf16[16,64,64,64]{3,2,1,0:T(8,128)(2,1)} %vol_ref.3, bf16[2,64,128]{2,1,0:T(8,128)(2,1)} %res_ref.3), custom_call_target="tpu_custom_call" | custom-call | tf_op jit(solution)/shard_map/render1/pallas_call | solution.py:141
  28.8 7.3 %all-to-all-start = ((bf16[32,2,72,128]{3,2,1,0:T(8,128)(2,1)}), bf16[32,2,72,128]{3,2,1,0:T(8,128)(2,1)S(1)}, u32[]{:S(2)}, u32[]{:S(2)}) async-start(bf16[32,2,72,128]{3,2,1,0:T(8,128)(2,1)} %bitcast.50), calls=%async_computation | async-start | bytes 2359296 | tf_op jit(solution)/shard_map/all_to_all | solution.py:226
  36.1 28.6 %render0.1 = bf16[64,64,128]{2,1,0:T(8,128)(2,1)} custom-call(f32[3]{0:T(128)} %slope_ref.3, f32[3]{0:T(128)} %pivot_ref.3, s32[1,128]{1,0:T(1,128)} %tile.12.code_ref, bf16[16,64,64,64]{3,2,1,0:T(8,128)(2,1)} %vol_ref.3, bf16[2,64,128]{2,1,0:T(8,128)(2,1)} %res_ref.3), custom_call_target="tpu_custom_call" | custom-call | tf_op jit(solution)/shard_map/render0/pallas_call | solution.py:141
  64.7 1.7 %all-to-all-done.got_ref = bf16[32,2,72,128]{3,2,1,0:T(8,128)(2,1)S(1)} async-done(((bf16[32,2,72,128]{3,2,1,0:T(8,128)(2,1)}), bf16[32,2,72,128]{3,2,1,0:T(8,128)(2,1)S(1)}, u32[]{:S(2)}, u32[]{:S(2)}) %all-to-all-start) | async-done | bytes 1179680 | tf_op jit(solution)/shard_map/all_to_all | solution.py:226
  66.4 4.1 %all-to-all-start.1 = ((bf16[32,2,64,128]{3,2,1,0:T(8,128)(2,1)}), bf16[32,2,64,128]{3,2,1,0:T(8,128)(2,1)S(1)}, u32[]{:S(2)}, u32[]{:S(2)}) async-start(bf16[32,2,64,128]{3,2,1,0:T(8,128)(2,1)} %bitcast.51), calls=%async_computation.1 | async-start | bytes 2097152 | tf_op jit(solution)/shard_map/all_to_all | solution.py:226
  71.0 0.7 slice.46.row_ref
  71.7 0.1 stack_squeeze.12
  71.8 0.7 slice.43.row_ref
  72.5 0.1 reshape.38
  72.6 0.9 copy.40.col_ref
  73.5 0.9 copy.41.col_ref
  74.3 3.7 %compose.2.refs_0_ = f32[64,2,8,128]{3,2,1,0:T(8,128)} custom-call(s32[1,512]{1,0:T(1,128)} %slice.46.row_ref, s32[512,2]{1,0:T(8,128)} %copy.40.col_ref, bf16[32,2,72,128]{3,2,1,0:T(8,128)(2,1)} %copy-done), custom_call_target="tpu_custom_call" | custom-call | tf_op jit(solution)/shard_map/compose/pallas_call | solution.py:209
  78.0 20.0 %all-to-all-done.1.got_ref = bf16[32,2,64,128]{3,2,1,0:T(8,128)(2,1)S(1)} async-done(((bf16[32,2,64,128]{3,2,1,0:T(8,128)(2,1)}), bf16[32,2,64,128]{3,2,1,0:T(8,128)(2,1)S(1)}, u32[]{:S(2)}, u32[]{:S(2)}) %all-to-all-start.1) | async-done | bytes 1048608 | tf_op jit(solution)/shard_map/all_to_all | solution.py:226
  98.0 1.0 copy-done.1
  99.0 3.6 %compose.3 = f32[64,2,8,128]{3,2,1,0:T(8,128)} custom-call(s32[1,512]{1,0:T(1,128)} %slice.43.row_ref, s32[512,2]{1,0:T(8,128)} %copy.41.col_ref, bf16[32,2,64,128]{3,2,1,0:T(8,128)(2,1)} %copy-done.1, f32[64,2,8,128]{3,2,1,0:T(8,128)} %compose.2.refs_0_), custom_call_target="tpu_custom_call", output_to_operand_aliasing={{}: (3, {})} | custom-call | tf_op jit(solution)/shard_map/compose/pallas_call | solution.py:209
  102.6 1.1 convert_element_type.23
  103.7 12.6 %all_to_all.15 = f16[32,4,8,128]{3,2,1,0:T(8,128)(2,1)S(1)} all-to-all(f16[32,4,8,128]{3,2,1,0:T(8,128)(2,1)S(1)} %bitcast.55), channel_id=1, replica_groups=mesh['depth'=4,'tile'=8] {'depth','tile'}, dimensions={0} | all-to-all | bytes 524288 | tf_op jit(solution)/shard_map/all_to_all | solution.py:226
  116.4 0.3 copy.42
  116.7 0.8 slice_bitcast_fusion
  117.4 0.7 slice_multiply_fusion
  (18 shorter events, 0.5 us)
Async XLA Ops:
  28.8 37.6 %all-to-all-start = ((bf16[32,2,72,128]{3,2,1,0:T(8,128)(2,1)}), bf16[32,2,72,128]{3,2,1,0:T(8,128)(2,1)S(1)}, u32[]{:S(2)}, u32[]{:S(2)}) async-start(bf16[32,2,72,128]{3,2,1,0:T(8,128)(2,1)} %bitcast.50), calls=%async_computation | async-start | bytes 2359296 | tf_op jit(solution)/shard_map/all_to_all | solution.py:226
  66.4 4.4 %copy-start = (bf16[32,2,72,128]{3,2,1,0:T(8,128)(2,1)}, bf16[32,2,72,128]{3,2,1,0:T(8,128)(2,1)S(1)}, u32[]{:S(2)}) copy-start(bf16[32,2,72,128]{3,2,1,0:T(8,128)(2,1)S(1)} %all-to-all-done.got_ref) | copy-start | bytes 3538948
  66.4 31.6 %all-to-all-start.1 = ((bf16[32,2,64,128]{3,2,1,0:T(8,128)(2,1)}), bf16[32,2,64,128]{3,2,1,0:T(8,128)(2,1)S(1)}, u32[]{:S(2)}, u32[]{:S(2)}) async-start(bf16[32,2,64,128]{3,2,1,0:T(8,128)(2,1)} %bitcast.51), calls=%async_computation.1 | async-start | bytes 2097152 | tf_op jit(solution)/shard_map/all_to_all | solution.py:226
  98.0 1.0 copy-start.1

commit v5 on v4

--- a/solution.py
+++ b/solution.py
@@ -15,7 +15,7 @@
 AXES = ("depth", "tile")
 
 
-def render_kernel(slope_ref, pivot_ref, code_ref, vol_ref, res_ref, out_ref, even_ref, odd_ref, ramp_ref, acc_ref, seen_ref, tint_ref, print_ref, *, view, count, tagged):
+def render_kernel(slope_ref, pivot_ref, owner_ref, cell_ref, order_ref, rank_ref, slab_ref, vol_ref, res_ref, out_ref, even_ref, odd_ref, ramp_ref, acc_ref, seen_ref, tint_ref, print_ref, *, view, count, tagged, tiles):
     step = pl.program_id(0)
     bricks = count
     edge = vol_ref.shape[1]
@@ -121,7 +121,20 @@
         finish(step - 1)
 
         if tagged:
-            code = jnp.broadcast_to(code_ref[...], (TAGS, cols))
+            views = order_ref.shape[0]
+            slabs = rank_ref.shape[1]
+            cells_each = CELLS // slabs
+            bricks_all = slabs * tiles * count
+            lane = lax.rem(lax.broadcasted_iota(jnp.int32, (TAGS, cols), 1), views * count)
+            code = jnp.zeros((TAGS, cols), jnp.int32)
+            for v in range(views):
+                rank = rank_ref[v, slab_ref[0]]
+                for b in range(count):
+                    cell = cell_ref[b, v]
+                    group = lax.div(cell, cells_each)
+                    place = (group * tiles + owner_ref[b, v]) * cells_each + (cell - group * cells_each)
+                    value = (place * slabs + rank) * bricks_all + order_ref[v, b]
+                    code = jnp.where(lane == v * count + b, value, code)
             digit = lax.broadcasted_iota(jnp.int32, (TAGS, cols), 0)
             tags = jnp.where(digit == 0, code & 255, jnp.where(digit == 1, (code >> 8) & 255, code >> 16)).astype(jnp.float32)
 
@@ -133,18 +146,18 @@
         lax.fori_loop(0, edge, swap, 0, unroll=4)
 
 
-def render(volume, resampler, slope, pivot, code, view, first, count, tagged):
+def render(volume, resampler, slope, pivot, tags, view, first, count, tagged):
     edge, cols = volume.shape[1], resampler.shape[2]
     pitch = edge + 1
     slots = 4 * count + (TAGS if tagged else 0)
     smem = pl.BlockSpec(memory_space=pltpu.SMEM)
     return pl.pallas_call(
-        functools.partial(render_kernel, view=view, count=count, tagged=tagged),
+        functools.partial(render_kernel, view=view, count=count, tagged=tagged, tiles=lax.axis_size("tile")),
         grid=(count + 1,),
         in_specs=[
             smem,
             smem,
-            pl.BlockSpec((1, cols), lambda g: (0, 0)),
+        ] + [smem] * len(tags) + [
             pl.BlockSpec((1, edge, edge, edge), lambda g: (first + jnp.minimum(g, count - 1), 0, 0, 0)),
             pl.BlockSpec((1, edge, cols), lambda g: (view, 0, 0)),
         ],
@@ -160,7 +173,7 @@
             pltpu.VMEM((4 * count * pitch, cols), jnp.float32),
         ],
         name=f"render{view}",
-    )(slope, pivot, code, volume, resampler)
+    )(slope, pivot, *tags, volume, resampler)
 
 
 def compose_kernel(row_ref, col_ref, got_ref, *refs, base, count):
@@ -170,8 +183,8 @@
     bands, width = got_ref.shape[1], got_ref.shape[3]
     for band in range(bands):
         for ch in range(4):
-            part = got_ref[:, band, ch * count:(ch + 1) * count, :].astype(jnp.float32)
-            feat_ref[ch, :, band * width:(band + 1) * width] = part.reshape(total, width).astype(jnp.bfloat16)
+            part = got_ref[:, band, ch * count:(ch + 1) * count, :]
+            feat_ref[ch, :, band * width:(band + 1) * width] = part.reshape(total, width)
     sum_ref[...] = jnp.zeros_like(sum_ref)
     block = min(256, total)
     row = row_ref[...]
@@ -218,6 +231,7 @@
             pltpu.VMEM((places, bands * 4, width), jnp.float32),
         ],
         input_output_aliases={3: 0} if more else {},
+        compiler_params=pltpu.CompilerParams(vmem_limit_bytes=32 << 20),
         name="compose",
     )(row, col, got, *more)
 
@@ -237,18 +251,14 @@
     bands, groups = max(1, edge // devices), max(1, devices // edge)
     width = cols // groups
 
-    rank = lax.dynamic_slice_in_dim(slab_rank, lax.axis_index("depth"), 1, 1)
-    key = rank * (devices * count) + depth_order
-    owner, cell = tile_owner.T, tile_cell.T
-    place = ((cell // cells_each) * tiles + owner) * cells_each + cell % cells_each
-    code = (place * base + key).reshape(1, views * count)
-    code = jnp.tile(code, (1, cols // (views * count)))
+    slab = lax.axis_index("depth").astype(jnp.int32).reshape(1)
+    tags = (tile_owner, tile_cell, depth_order, slab_rank, slab)
 
     order = list(range(views))[::-1]
     made, codes = None, None
     for view in order:
         tagged = view == order[0]
-        prints = render(volume, resampler, ramp_slope, ramp_pivot, code, view, 0, count, tagged)
+        prints = render(volume, resampler, ramp_slope, ramp_pivot, tags, view, 0, count, tagged)
         prints = prints.reshape(edge, -1, groups, width).transpose(0, 2, 1, 3)
         got = exchange(prints.reshape(devices, bands, -1, width))
         if tagged:

time: 119 us -> 115 us (0.966)
  waiting for transfers between devices: 21.7 us -> 26.3 us
  Pallas kernels: 61.7 us -> 57.8 us
  other arithmetic: 3.54 us -> 0.85 us
  local copies, waits for them, and re-layouts: 6.34 us -> 4.78 us
    all_to_all x2, waiting for transfers between devices: 21.7 us -> 26.3 us  [exchange(): return lax.all_to_all(parts, AXES, split_axis=0, concat_axis=0, tiled=True)]
    pallas_call x2, Pallas kernels: 7.32 us -> 3.19 us  [compose(): pl.pallas_call(functools.partial(compose_kernel, base=base, count=count),...]
    unnamed x4 -> x2, local copies, waits for them, and re-layouts: 0.98 us -> 2.71 us
    another operation x5, local copies, waits for them, and re-layouts: 1.9 us -> 0.46 us  [body(): col = jnp.stack([codes[view], floors[view]], axis=1)]
  transfers between devices with their start and end apart: 2 -> 2, of which waited for: 2 -> 2; matrix products, arithmetic and copies ran while one was open for 3% -> 1% of each run, Pallas kernels for 27% -> 26%
where the time goes in v5:
time: 115 us
  Pallas kernels  57.8 us (50%)
  waiting for transfers between devices  26.3 us (23%)
  blocking collectives  12.6 us (11%)
  starting transfers between devices  11.5 us (10%)
  local copies, waits for them, and re-layouts  4.78 us (4%)
    pallas_call x2, Pallas kernels, render(): pl.pallas_call(functools.partial(render_kernel, view=view, count=count, t...  54.6 us
    all_to_all x2, waiting for transfers between devices, exchange(): return lax.all_to_all(parts, AXES, split_axis=0, concat_axis=0, tiled=True)  26.3 us
    all_to_all x1, blocking collectives, exchange(): return lax.all_to_all(parts, AXES, split_axis=0, concat_axis=0, tiled=True)  12.6 us
    all_to_all x2, starting transfers between devices, exchange(): return lax.all_to_all(parts, AXES, split_axis=0, concat_axis=0, tiled=True)  11.5 us
    pallas_call x2, Pallas kernels, compose(): pl.pallas_call(functools.partial(compose_kernel, base=base, count=count),...  3.19 us
    unnamed x2, local copies, waits for them, and re-layouts  2.71 us
  transfers between devices with their start and end apart: 2, of which 2 were waited for; matrix products, arithmetic and copies ran while one was open for 1% of the time, Pallas kernels for 26%

profile of v5, /device:TPU:0, one launch (start us, length us, event | category | flops | bytes accessed | tf_op | source)
XLA Modules:
  0.0 114.7 jit_solution(15221209142100621074)
XLA Ops:
  0.6 1.4 %copy.45.owner_ref = s32[16,2]{1,0:T(8,128)} copy(s32[16,2]{0,1:T(2,128)} %param.12) | data formatting | bytes 256 | tf_op args[4]
  2.0 1.4 %copy.46.cell_ref = s32[16,2]{1,0:T(8,128)} copy(s32[16,2]{0,1:T(2,128)} %param.13) | data formatting | bytes 256 | tf_op args[5]
  3.3 26.0 %render1.1 = bf16[64,72,128]{2,1,0:T(8,128)(2,1)} custom-call(f32[3]{0:T(128)} %slope_ref.3, f32[3]{0:T(128)} %pivot_ref.3, s32[16,2]{1,0:T(8,128)} %copy.45.owner_ref, s32[16,2]{1,0:T(8,128)} %copy.46.cell_ref, s32[2,16]{1,0:T(2,128)} %order_ref.3, s32[2,4]{1,0:T(2,128)} %rank_ref.3, s32[1]{0:T(128)} %bitcast.slab_ref, bf16[16,64,64,64]{3,2,1,0:T(8,128)(2,1)} %vol_ref.3, ...), custom_call_target="tpu_custom_call" | custom-call | tf_op jit(solution)/shard_map/render1/pallas_call | solution.py:154
  29.4 7.3 %all-to-all-start = ((bf16[32,2,72,128]{3,2,1,0:T(8,128)(2,1)}), bf16[32,2,72,128]{3,2,1,0:T(8,128)(2,1)S(1)}, u32[]{:S(2)}, u32[]{:S(2)}) async-start(bf16[32,2,72,128]{3,2,1,0:T(8,128)(2,1)} %bitcast.27), calls=%async_computation | async-start | bytes 2359296 | tf_op jit(solution)/shard_map/all_to_all | solution.py:240
  36.7 28.6 %render0.1 = bf16[64,64,128]{2,1,0:T(8,128)(2,1)} custom-call(f32[3]{0:T(128)} %slope_ref.3, f32[3]{0:T(128)} %pivot_ref.3, s32[16,2]{1,0:T(8,128)} %copy.45.owner_ref, s32[16,2]{1,0:T(8,128)} %copy.46.cell_ref, s32[2,16]{1,0:T(2,128)} %order_ref.3, s32[2,4]{1,0:T(2,128)} %rank_ref.3, s32[1]{0:T(128)} %bitcast.slab_ref, bf16[16,64,64,64]{3,2,1,0:T(8,128)(2,1)} %vol_ref.3, ...), custom_call_target="tpu_custom_call" | custom-call | tf_op jit(solution)/shard_map/render0/pallas_call | solution.py:154
  65.3 1.7 %all-to-all-done.got_ref = bf16[32,2,72,128]{3,2,1,0:T(8,128)(2,1)S(1)} async-done(((bf16[32,2,72,128]{3,2,1,0:T(8,128)(2,1)}), bf16[32,2,72,128]{3,2,1,0:T(8,128)(2,1)S(1)}, u32[]{:S(2)}, u32[]{:S(2)}) %all-to-all-start) | async-done | bytes 1179680 | tf_op jit(solution)/shard_map/all_to_all | solution.py:240
  67.0 4.2 %all-to-all-start.1 = ((bf16[32,2,64,128]{3,2,1,0:T(8,128)(2,1)}), bf16[32,2,64,128]{3,2,1,0:T(8,128)(2,1)S(1)}, u32[]{:S(2)}, u32[]{:S(2)}) async-start(bf16[32,2,64,128]{3,2,1,0:T(8,128)(2,1)} %bitcast.28), calls=%async_computation.1 | async-start | bytes 2097152 | tf_op jit(solution)/shard_map/all_to_all | solution.py:240
  71.3 0.1 copy.51
  71.4 0.1 copy.54
  71.5 0.1 stack_squeeze.14
  71.6 0.1 slice.46.row_ref
  71.6 0.1 copy.49
  71.7 0.1 stack_squeeze.12
  71.8 0.1 slice.43.row_ref
  71.9 0.1 reshape.36
  72.0 0.1 copy.56.col_ref
  72.2 0.1 copy.57.col_ref
  72.4 1.6 %compose.2.refs_0_ = f32[64,2,8,128]{3,2,1,0:T(8,128)S(1)} custom-call(s32[1,512]{1,0:T(1,128)S(1)} %slice.46.row_ref, s32[512,2]{1,0:T(8,128)S(1)} %copy.56.col_ref, bf16[32,2,72,128]{3,2,1,0:T(8,128)(2,1)S(1)} %all-to-all-done.got_ref), custom_call_target="tpu_custom_call" | custom-call | tf_op jit(solution)/shard_map/compose/pallas_call | solution.py:222
  74.0 24.7 %all-to-all-done.1.got_ref = bf16[32,2,64,128]{3,2,1,0:T(8,128)(2,1)S(1)} async-done(((bf16[32,2,64,128]{3,2,1,0:T(8,128)(2,1)}), bf16[32,2,64,128]{3,2,1,0:T(8,128)(2,1)S(1)}, u32[]{:S(2)}, u32[]{:S(2)}) %all-to-all-start.1) | async-done | bytes 1048608 | tf_op jit(solution)/shard_map/all_to_all | solution.py:240
  98.6 1.6 %compose.3 = f32[64,2,8,128]{3,2,1,0:T(8,128)S(1)} custom-call(s32[1,512]{1,0:T(1,128)S(1)} %slice.43.row_ref, s32[512,2]{1,0:T(8,128)S(1)} %copy.57.col_ref, bf16[32,2,64,128]{3,2,1,0:T(8,128)(2,1)S(1)} %all-to-all-done.1.got_ref, f32[64,2,8,128]{3,2,1,0:T(8,128)S(1)} %compose.2.refs_0_), custom_call_target="tpu_custom_call", output_to_operand_aliasing={{}: (3, {})} | custom-call | tf_op jit(solution)/shard_map/compose/pallas_call | solution.py:222
  100.3 12.6 %all_to_all.15 = f16[32,4,8,128]{3,2,1,0:T(8,128)(2,1)S(1)} all-to-all(f16[32,4,8,128]{3,2,1,0:T(8,128)(2,1)S(1)} %bitcast.32), channel_id=1, replica_groups=mesh['depth'=4,'tile'=8] {'depth','tile'}, dimensions={0} | all-to-all | bytes 524288 | tf_op jit(solution)/shard_map/all_to_all | solution.py:240
  112.9 0.3 copy.58
  113.2 0.8 slice_bitcast_fusion
  114.0 0.7 slice_multiply_fusion
  (11 shorter events, 0.3 us)
Async XLA Ops:
  29.4 37.6 %all-to-all-start = ((bf16[32,2,72,128]{3,2,1,0:T(8,128)(2,1)}), bf16[32,2,72,128]{3,2,1,0:T(8,128)(2,1)S(1)}, u32[]{:S(2)}, u32[]{:S(2)}) async-start(bf16[32,2,72,128]{3,2,1,0:T(8,128)(2,1)} %bitcast.27), calls=%async_computation | async-start | bytes 2359296 | tf_op jit(solution)/shard_map/all_to_all | solution.py:240
  67.0 31.6 %all-to-all-start.1 = ((bf16[32,2,64,128]{3,2,1,0:T(8,128)(2,1)}), bf16[32,2,64,128]{3,2,1,0:T(8,128)(2,1)S(1)}, u32[]{:S(2)}, u32[]{:S(2)}) async-start(bf16[32,2,64,128]{3,2,1,0:T(8,128)(2,1)} %bitcast.28), calls=%async_computation.1 | async-start | bytes 2097152 | tf_op jit(solution)/shard_map/all_to_all | solution.py:240

commit v6 on v5

--- a/solution.py
+++ b/solution.py
@@ -15,7 +15,7 @@
 AXES = ("depth", "tile")
 
 
-def render_kernel(slope_ref, pivot_ref, owner_ref, cell_ref, order_ref, rank_ref, slab_ref, vol_ref, res_ref, out_ref, even_ref, odd_ref, ramp_ref, acc_ref, seen_ref, tint_ref, print_ref, *, view, count, tagged, tiles):
+def render_kernel(slope_ref, pivot_ref, owner_ref, cell_ref, order_ref, rank_ref, slab_ref, vol_ref, res_ref, out_ref, even_ref, odd_ref, ramp_ref, acc_ref, seen_ref, tint_ref, print_ref, *, view, count, tagged, tiles, bands):
     step = pl.program_id(0)
     bricks = count
     edge = vol_ref.shape[1]
@@ -130,29 +130,31 @@
             for v in range(views):
                 rank = rank_ref[v, slab_ref[0]]
                 for b in range(count):
-                    cell = cell_ref[b, v]
+                    cell = cell_ref[v, b]
                     group = lax.div(cell, cells_each)
-                    place = (group * tiles + owner_ref[b, v]) * cells_each + (cell - group * cells_each)
+                    place = (group * tiles + owner_ref[v, b]) * cells_each + (cell - group * cells_each)
                     value = (place * slabs + rank) * bricks_all + order_ref[v, b]
                     code = jnp.where(lane == v * count + b, value, code)
             digit = lax.broadcasted_iota(jnp.int32, (TAGS, cols), 0)
             tags = jnp.where(digit == 0, code & 255, jnp.where(digit == 1, (code >> 8) & 255, code >> 16)).astype(jnp.float32)
 
         def swap(row, carry):
-            out_ref[row, :4 * bricks, :] = print_ref[pl.ds(row, 4 * bricks, stride=pitch), :].astype(jnp.bfloat16)
+            for band in range(bands):
+                part = print_ref[pl.ds(row * bands + band, 4 * bricks, stride=pitch), :]
+                out_ref[row, band * 4 * bricks:(band + 1) * 4 * bricks, :] = part.astype(jnp.bfloat16)
             if tagged:
-                out_ref[row, 4 * bricks:, :] = tags.astype(jnp.bfloat16)
+                out_ref[row, bands * 4 * bricks:, :] = tags.astype(jnp.bfloat16)
             return carry
-        lax.fori_loop(0, edge, swap, 0, unroll=4)
-
-
-def render(volume, resampler, slope, pivot, tags, view, first, count, tagged):
+        lax.fori_loop(0, edge // bands, swap, 0, unroll=2)
+
+
+def render(volume, resampler, slope, pivot, tags, view, first, count, bands, tagged):
     edge, cols = volume.shape[1], resampler.shape[2]
     pitch = edge + 1
-    slots = 4 * count + (TAGS if tagged else 0)
+    slots = bands * 4 * count + (TAGS if tagged else 0)
     smem = pl.BlockSpec(memory_space=pltpu.SMEM)
     return pl.pallas_call(
-        functools.partial(render_kernel, view=view, count=count, tagged=tagged, tiles=lax.axis_size("tile")),
+        functools.partial(render_kernel, view=view, count=count, tagged=tagged, tiles=lax.axis_size("tile"), bands=bands),
         grid=(count + 1,),
         in_specs=[
             smem,
@@ -161,8 +163,8 @@
             pl.BlockSpec((1, edge, edge, edge), lambda g: (first + jnp.minimum(g, count - 1), 0, 0, 0)),
             pl.BlockSpec((1, edge, cols), lambda g: (view, 0, 0)),
         ],
-        out_specs=pl.BlockSpec((edge, slots, cols), lambda g: (0, 0, 0)),
-        out_shape=jax.ShapeDtypeStruct((edge, slots, cols), jnp.bfloat16),
+        out_specs=pl.BlockSpec((edge // bands, slots, cols), lambda g: (0, 0, 0)),
+        out_shape=jax.ShapeDtypeStruct((edge // bands, slots, cols), jnp.bfloat16),
         scratch_shapes=[
             pltpu.VMEM((edge * pitch, cols), jnp.float32),
             pltpu.VMEM((edge * pitch, cols), jnp.float32),
@@ -180,10 +182,12 @@
     out_ref, feat_ref, sum_ref, pack_ref = refs[-4:]
     total, lanes = feat_ref.shape[1:]
     places = sum_ref.shape[1]
-    bands, width = got_ref.shape[1], got_ref.shape[3]
+    width = got_ref.shape[2]
+    bands = lanes // width
     for band in range(bands):
         for ch in range(4):
-            part = got_ref[:, band, ch * count:(ch + 1) * count, :]
+            first = (band * 4 + ch) * count
+            part = got_ref[:, first:first + count, :]
             feat_ref[ch, :, band * width:(band + 1) * width] = part.reshape(total, width)
     sum_ref[...] = jnp.zeros_like(sum_ref)
     block = min(256, total)
@@ -214,8 +218,8 @@
     out_ref[:, 0] = pack_ref[...].astype(out_ref.dtype)
 
 
-def compose(row, col, got, made, view, views, count, places, base):
-    sources, bands, slots, width = got.shape
+def compose(row, col, got, made, view, views, count, bands, places, base):
+    width = got.shape[2]
     total = row.shape[1]
     more = [] if made is None else [made]
     vmem = pl.BlockSpec(memory_space=pltpu.VMEM)
@@ -252,22 +256,22 @@
     width = cols // groups
 
     slab = lax.axis_index("depth").astype(jnp.int32).reshape(1)
-    tags = (tile_owner, tile_cell, depth_order, slab_rank, slab)
+    tags = (tile_owner.T, tile_cell.T, depth_order, slab_rank, slab)
 
     order = list(range(views))[::-1]
     made, codes = None, None
     for view in order:
         tagged = view == order[0]
-        prints = render(volume, resampler, ramp_slope, ramp_pivot, tags, view, 0, count, tagged)
-        prints = prints.reshape(edge, -1, groups, width).transpose(0, 2, 1, 3)
-        got = exchange(prints.reshape(devices, bands, -1, width))
+        prints = render(volume, resampler, ramp_slope, ramp_pivot, tags, view, 0, count, bands, tagged)
+        prints = prints.reshape(edge // bands, -1, groups, width).transpose(0, 2, 1, 3)
+        got = exchange(prints.reshape(devices, -1, width))
         if tagged:
-            digits = got[:, 0, 4 * count:4 * count + 3, :views * count].astype(jnp.int32)
+            digits = got[:, bands * 4 * count:bands * 4 * count + 3, :views * count].astype(jnp.int32)
             codes = digits[:, 0] + digits[:, 1] * 256 + digits[:, 2] * 65536
             codes = codes.reshape(devices, views, count).transpose(1, 0, 2).reshape(views, -1)
             floors = (codes // base) * base
         col = jnp.stack([codes[view], floors[view]], axis=1)
-        made = compose(codes[view][None], col, got, made, view, views, count, places, base)
+        made = compose(codes[view][None], col, got, made, view, views, count, bands, places, base)
     final = exchange(made.astype(jnp.float16).reshape(devices, cells_each * views, bands * 4, width))
     final = final.reshape(edge // bands, groups, cells_each, views, bands, 4, width)
     final = final.transpose(3, 5, 2, 0, 4, 1, 6).reshape(views, 4, cells_each * edge, cols)

time: 115 us -> 112 us (0.974)
  local copies, waits for them, and re-layouts: 4.78 us -> 2.07 us
  waiting for transfers between devices: 26.3 us -> 24.9 us
  starting transfers between devices: 11.5 us -> 12.9 us
    unnamed x2 -> x0, local copies, waits for them, and re-layouts: 2.71 us -> none
    all_to_all x2, starting transfers between devices: 11.5 us -> 12.9 us  [exchange(): return lax.all_to_all(parts, AXES, split_axis=0, concat_axis=0, tiled=True)]
    all_to_all x2, waiting for transfers between devices: 26.3 us -> 24.9 us  [exchange(): return lax.all_to_all(parts, AXES, split_axis=0, concat_axis=0, tiled=True)]
  transfers between devices with their start and end apart: 2 -> 2, of which waited for: 2 -> 2; matrix products, arithmetic and copies ran while one was open for 1% -> 1% of each run, Pallas kernels for 26% -> 27%
where the time goes in v6:
time: 112 us
  Pallas kernels  57.9 us (52%)
  waiting for transfers between devices  24.9 us (22%)
  starting transfers between devices  12.9 us (12%)
  blocking collectives  12.6 us (11%)
  local copies, waits for them, and re-layouts  2.07 us (2%)
    pallas_call x2, Pallas kernels, render(): pl.pallas_call(functools.partial(render_kernel, view=view, count=count, t...  54.7 us
    all_to_all x2, waiting for transfers between devices, exchange(): return lax.all_to_all(parts, AXES, split_axis=0, concat_axis=0, tiled=True)  24.9 us
    all_to_all x2, starting transfers between devices, exchange(): return lax.all_to_all(parts, AXES, split_axis=0, concat_axis=0, tiled=True)  12.9 us
    all_to_all x1, blocking collectives, exchange(): return lax.all_to_all(parts, AXES, split_axis=0, concat_axis=0, tiled=True)  12.6 us
    pallas_call x2, Pallas kernels, compose(): pl.pallas_call(functools.partial(compose_kernel, base=base, count=count),...  3.19 us
  transfers between devices with their start and end apart: 2, of which 2 were waited for; matrix products, arithmetic and copies ran while one was open for 1% of the time, Pallas kernels for 27%

profile of v6, /device:TPU:0, one launch (start us, length us, event | category | flops | bytes accessed | tf_op | source)
XLA Modules:
  0.0 112.0 jit_solution(16066588652406354427)
XLA Ops:
  0.6 26.0 %render1.1 = bf16[32,136,128]{2,1,0:T(8,128)(2,1)} custom-call(f32[3]{0:T(128)} %slope_ref.3, f32[3]{0:T(128)} %pivot_ref.3, s32[2,16]{1,0:T(2,128)} %bitcast.29, s32[2,16]{1,0:T(2,128)} %bitcast.31, s32[2,16]{1,0:T(2,128)} %order_ref.3, s32[2,4]{1,0:T(2,128)} %rank_ref.3, s32[1]{0:T(128)} %bitcast.2.slab_ref, bf16[16,64,64,64]{3,2,1,0:T(8,128)(2,1)} %vol_ref.3, ...), custom_call_target="tpu_custom_call" | custom-call | tf_op jit(solution)/shard_map/render1/pallas_call | solution.py:156
  26.7 7.3 %all-to-all-start = ((bf16[32,136,128]{2,1,0:T(8,128)(2,1)}), bf16[32,136,128]{2,1,0:T(8,128)(2,1)S(1)}, u32[]{:S(2)}, u32[]{:S(2)}) async-start(bf16[32,136,128]{2,1,0:T(8,128)(2,1)} %render1.1), calls=%async_computation | async-start | bytes 2228224 | tf_op jit(solution)/shard_map/all_to_all | solution.py:244
  34.0 28.7 %render0.1 = bf16[32,128,128]{2,1,0:T(8,128)(2,1)} custom-call(f32[3]{0:T(128)} %slope_ref.3, f32[3]{0:T(128)} %pivot_ref.3, s32[2,16]{1,0:T(2,128)} %bitcast.30, s32[2,16]{1,0:T(2,128)} %bitcast.32, s32[2,16]{1,0:T(2,128)} %order_ref.3, s32[2,4]{1,0:T(2,128)} %rank_ref.3, s32[1]{0:T(128)} %bitcast.2.slab_ref, bf16[16,64,64,64]{3,2,1,0:T(8,128)(2,1)} %vol_ref.3, ...), custom_call_target="tpu_custom_call" | custom-call | tf_op jit(solution)/shard_map/render0/pallas_call | solution.py:156
  62.7 0.2 all-to-all-done.got_ref
  62.9 5.6 %all-to-all-start.1 = ((bf16[32,128,128]{2,1,0:T(8,128)(2,1)}), bf16[32,128,128]{2,1,0:T(8,128)(2,1)S(1)}, u32[]{:S(2)}, u32[]{:S(2)}) async-start(bf16[32,128,128]{2,1,0:T(8,128)(2,1)} %render0.1), calls=%async_computation.1 | async-start | bytes 2097152 | tf_op jit(solution)/shard_map/all_to_all | solution.py:244
  68.6 0.1 copy.34
  68.7 0.1 copy.37
  68.8 0.1 copy.38
  68.8 0.1 stack_squeeze.14
  68.9 0.1 slice.46.row_ref
  69.0 0.1 copy.35
  69.1 0.1 stack_squeeze.12
  69.2 0.1 slice.43.row_ref
  69.2 0.1 reshape.34
  69.4 0.1 copy.40.col_ref
  69.6 0.1 copy.41.col_ref
  69.7 1.6 %compose.2.refs_0_ = f32[64,2,8,128]{3,2,1,0:T(8,128)S(1)} custom-call(s32[1,512]{1,0:T(1,128)S(1)} %slice.46.row_ref, s32[512,2]{1,0:T(8,128)S(1)} %copy.40.col_ref, bf16[32,136,128]{2,1,0:T(8,128)(2,1)S(1)} %all-to-all-done.got_ref), custom_call_target="tpu_custom_call" | custom-call | tf_op jit(solution)/shard_map/compose/pallas_call | solution.py:226
  71.3 24.7 %all-to-all-done.1.got_ref = bf16[32,128,128]{2,1,0:T(8,128)(2,1)S(1)} async-done(((bf16[32,128,128]{2,1,0:T(8,128)(2,1)}), bf16[32,128,128]{2,1,0:T(8,128)(2,1)S(1)}, u32[]{:S(2)}, u32[]{:S(2)}) %all-to-all-start.1) | async-done | bytes 1048608 | tf_op jit(solution)/shard_map/all_to_all | solution.py:244
  96.0 1.6 %compose.3 = f32[64,2,8,128]{3,2,1,0:T(8,128)S(1)} custom-call(s32[1,512]{1,0:T(1,128)S(1)} %slice.43.row_ref, s32[512,2]{1,0:T(8,128)S(1)} %copy.41.col_ref, bf16[32,128,128]{2,1,0:T(8,128)(2,1)S(1)} %all-to-all-done.1.got_ref, f32[64,2,8,128]{3,2,1,0:T(8,128)S(1)} %compose.2.refs_0_), custom_call_target="tpu_custom_call", output_to_operand_aliasing={{}: (3, {})} | custom-call | tf_op jit(solution)/shard_map/compose/pallas_call | solution.py:226
  97.6 12.6 %all_to_all.15 = f16[32,4,8,128]{3,2,1,0:T(8,128)(2,1)S(1)} all-to-all(f16[32,4,8,128]{3,2,1,0:T(8,128)(2,1)S(1)} %bitcast.25), channel_id=1, replica_groups=mesh['depth'=4,'tile'=8] {'depth','tile'}, dimensions={0} | all-to-all | bytes 524288 | tf_op jit(solution)/shard_map/all_to_all | solution.py:244
  110.2 0.1 convert.6
  110.3 0.3 copy.42
  110.6 0.8 slice_bitcast_fusion
  111.3 0.7 slice_multiply_fusion
  (9 shorter events, 0.1 us)
Async XLA Ops:
  26.7 36.2 %all-to-all-start = ((bf16[32,136,128]{2,1,0:T(8,128)(2,1)}), bf16[32,136,128]{2,1,0:T(8,128)(2,1)S(1)}, u32[]{:S(2)}, u32[]{:S(2)}) async-start(bf16[32,136,128]{2,1,0:T(8,128)(2,1)} %render1.1), calls=%async_computation | async-start | bytes 2228224 | tf_op jit(solution)/shard_map/all_to_all | solution.py:244
  62.9 33.1 %all-to-all-start.1 = ((bf16[32,128,128]{2,1,0:T(8,128)(2,1)}), bf16[32,128,128]{2,1,0:T(8,128)(2,1)S(1)}, u32[]{:S(2)}, u32[]{:S(2)}) async-start(bf16[32,128,128]{2,1,0:T(8,128)(2,1)} %render0.1), calls=%async_computation.1 | async-start | bytes 2097152 | tf_op jit(solution)/shard_map/all_to_all | solution.py:244

commit v7 on v6

--- a/solution.py
+++ b/solution.py
@@ -59,7 +59,9 @@
         for top in range(0, edge, strip):
             acc = acc_ref[pl.ds(top, strip), :]
             seen = seen_ref[pl.ds(top, strip), :]
-            part = [[] for _ in range(3)]
+            total = [None] * 3
+            held = [None] * 3
+            late = None
             for j in range(GROUP):
                 if view == 0:
                     s = samp_ref[pl.ds((block * GROUP + j) * edge + top, strip), :]
@@ -70,19 +72,24 @@
                 w = (seen - left).astype(jnp.bfloat16)
                 seen = left
                 s16 = s.astype(jnp.bfloat16)
-                for ch in range(3):
-                    gain = jnp.concatenate([ramp_ref[j, ch, 0]] * (strip // 16), axis=0)
-                    offset = jnp.concatenate([ramp_ref[j, ch, 1]] * (strip // 16), axis=0)
-                    p = w * jnp.tanh(s16 * gain + offset)
-                    n = j
-                    while n % 2 == 1:
-                        p = part[ch].pop() + p
-                        n //= 2
-                    part[ch].append(p)
+                tints = [jnp.tanh(s16 * ramp_ref[j, ch, 0] + ramp_ref[j, ch, 1]) for ch in range(3)]
+                if late is not None:
+                    take(total, held, j - 1, *late)
+                late = (w, tints)
+            take(total, held, GROUP - 1, *late)
             for ch in range(3):
-                tint_ref[ch, pl.ds(top, strip), :] += part[ch][0].astype(jnp.float32)
+                tint_ref[ch, pl.ds(top, strip), :] += total[ch].astype(jnp.float32)
             acc_ref[pl.ds(top, strip), :] = acc
             seen_ref[pl.ds(top, strip), :] = seen
+
+    def take(total, held, j, w, tints):
+        for ch in range(3):
+            p = w * tints[ch]
+            if j % 2 == 0:
+                held[ch] = p
+            else:
+                p = held[ch] + p
+                total[ch] = p if total[ch] is None else total[ch] + p
 
     def finish(brick):
         alpha = 1.0 - seen_ref[...]

time: 112 us -> 112 us (level)
  no operation moved by 1% of the time
where the time goes in v7:
time: 112 us; the launch traced here: 111 us
  Pallas kernels  57 us (51%)
  waiting for transfers between devices  25.4 us (23%)
  blocking collectives  12.6 us (11%)
  starting transfers between devices  12.5 us (11%)
  local copies, waits for them, and re-layouts  2.07 us (2%)
    pallas_call x2, Pallas kernels, render(): pl.pallas_call(functools.partial(render_kernel, view=view, count=count, t...  53.8 us
    all_to_all x2, waiting for transfers between devices, exchange(): return lax.all_to_all(parts, AXES, split_axis=0, concat_axis=0, tiled=True)  25.4 us
    all_to_all x1, blocking collectives, exchange(): return lax.all_to_all(parts, AXES, split_axis=0, concat_axis=0, tiled=True)  12.6 us
    all_to_all x2, starting transfers between devices, exchange(): return lax.all_to_all(parts, AXES, split_axis=0, concat_axis=0, tiled=True)  12.5 us
    pallas_call x2, Pallas kernels, compose(): pl.pallas_call(functools.partial(compose_kernel, base=base, count=count),...  3.19 us
  transfers between devices with their start and end apart: 2, of which 2 were waited for; matrix products, arithmetic and copies ran while one was open for 1% of the time, Pallas kernels for 27%

profile of v7, /device:TPU:0, one launch (start us, length us, event | category | flops | bytes accessed | tf_op | source)
XLA Modules:
  0.0 111.1 jit_solution(14116350069616798613)
XLA Ops:
  0.6 25.6 %render1.1 = bf16[32,136,128]{2,1,0:T(8,128)(2,1)} custom-call(f32[3]{0:T(128)} %slope_ref.3, f32[3]{0:T(128)} %pivot_ref.3, s32[2,16]{1,0:T(2,128)} %bitcast.29, s32[2,16]{1,0:T(2,128)} %bitcast.31, s32[2,16]{1,0:T(2,128)} %order_ref.3, s32[2,4]{1,0:T(2,128)} %rank_ref.3, s32[1]{0:T(128)} %bitcast.2.slab_ref, bf16[16,64,64,64]{3,2,1,0:T(8,128)(2,1)} %vol_ref.3, ...), custom_call_target="tpu_custom_call" | custom-call | tf_op jit(solution)/shard_map/render1/pallas_call | solution.py:163
  26.3 7.3 %all-to-all-start = ((bf16[32,136,128]{2,1,0:T(8,128)(2,1)}), bf16[32,136,128]{2,1,0:T(8,128)(2,1)S(1)}, u32[]{:S(2)}, u32[]{:S(2)}) async-start(bf16[32,136,128]{2,1,0:T(8,128)(2,1)} %render1.1), calls=%async_computation | async-start | bytes 2228224 | tf_op jit(solution)/shard_map/all_to_all | solution.py:251
  33.6 28.2 %render0.1 = bf16[32,128,128]{2,1,0:T(8,128)(2,1)} custom-call(f32[3]{0:T(128)} %slope_ref.3, f32[3]{0:T(128)} %pivot_ref.3, s32[2,16]{1,0:T(2,128)} %bitcast.30, s32[2,16]{1,0:T(2,128)} %bitcast.32, s32[2,16]{1,0:T(2,128)} %order_ref.3, s32[2,4]{1,0:T(2,128)} %rank_ref.3, s32[1]{0:T(128)} %bitcast.2.slab_ref, bf16[16,64,64,64]{3,2,1,0:T(8,128)(2,1)} %vol_ref.3, ...), custom_call_target="tpu_custom_call" | custom-call | tf_op jit(solution)/shard_map/render0/pallas_call | solution.py:163
  61.8 0.7 all-to-all-done.got_ref
  62.5 5.2 %all-to-all-start.1 = ((bf16[32,128,128]{2,1,0:T(8,128)(2,1)}), bf16[32,128,128]{2,1,0:T(8,128)(2,1)S(1)}, u32[]{:S(2)}, u32[]{:S(2)}) async-start(bf16[32,128,128]{2,1,0:T(8,128)(2,1)} %render0.1), calls=%async_computation.1 | async-start | bytes 2097152 | tf_op jit(solution)/shard_map/all_to_all | solution.py:251
  67.7 0.1 copy.34
  67.8 0.1 copy.37
  67.9 0.1 copy.38
  68.0 0.1 stack_squeeze.14
  68.0 0.1 slice.46.row_ref
  68.1 0.1 copy.35
  68.2 0.1 stack_squeeze.12
  68.3 0.1 slice.43.row_ref
  68.4 0.1 reshape.34
  68.5 0.1 copy.40.col_ref
  68.7 0.1 copy.41.col_ref
  68.8 1.6 %compose.2.refs_0_ = f32[64,2,8,128]{3,2,1,0:T(8,128)S(1)} custom-call(s32[1,512]{1,0:T(1,128)S(1)} %slice.46.row_ref, s32[512,2]{1,0:T(8,128)S(1)} %copy.40.col_ref, bf16[32,136,128]{2,1,0:T(8,128)(2,1)S(1)} %all-to-all-done.got_ref), custom_call_target="tpu_custom_call" | custom-call | tf_op jit(solution)/shard_map/compose/pallas_call | solution.py:233
  70.5 24.7 %all-to-all-done.1.got_ref = bf16[32,128,128]{2,1,0:T(8,128)(2,1)S(1)} async-done(((bf16[32,128,128]{2,1,0:T(8,128)(2,1)}), bf16[32,128,128]{2,1,0:T(8,128)(2,1)S(1)}, u32[]{:S(2)}, u32[]{:S(2)}) %all-to-all-start.1) | async-done | bytes 1048608 | tf_op jit(solution)/shard_map/all_to_all | solution.py:251
  95.1 1.6 %compose.3 = f32[64,2,8,128]{3,2,1,0:T(8,128)S(1)} custom-call(s32[1,512]{1,0:T(1,128)S(1)} %slice.43.row_ref, s32[512,2]{1,0:T(8,128)S(1)} %copy.41.col_ref, bf16[32,128,128]{2,1,0:T(8,128)(2,1)S(1)} %all-to-all-done.1.got_ref, f32[64,2,8,128]{3,2,1,0:T(8,128)S(1)} %compose.2.refs_0_), custom_call_target="tpu_custom_call", output_to_operand_aliasing={{}: (3, {})} | custom-call | tf_op jit(solution)/shard_map/compose/pallas_call | solution.py:233
  96.8 12.6 %all_to_all.15 = f16[32,4,8,128]{3,2,1,0:T(8,128)(2,1)S(1)} all-to-all(f16[32,4,8,128]{3,2,1,0:T(8,128)(2,1)S(1)} %bitcast.25), channel_id=1, replica_groups=mesh['depth'=4,'tile'=8] {'depth','tile'}, dimensions={0} | all-to-all | bytes 524288 | tf_op jit(solution)/shard_map/all_to_all | solution.py:251
  109.4 0.1 convert.6
  109.4 0.3 copy.42
  109.7 0.8 slice_bitcast_fusion
  110.5 0.7 slice_multiply_fusion
  (9 shorter events, 0.1 us)
Async XLA Ops:
  26.3 36.2 %all-to-all-start = ((bf16[32,136,128]{2,1,0:T(8,128)(2,1)}), bf16[32,136,128]{2,1,0:T(8,128)(2,1)S(1)}, u32[]{:S(2)}, u32[]{:S(2)}) async-start(bf16[32,136,128]{2,1,0:T(8,128)(2,1)} %render1.1), calls=%async_computation | async-start | bytes 2228224 | tf_op jit(solution)/shard_map/all_to_all | solution.py:251
  62.5 32.6 %all-to-all-start.1 = ((bf16[32,128,128]{2,1,0:T(8,128)(2,1)}), bf16[32,128,128]{2,1,0:T(8,128)(2,1)S(1)}, u32[]{:S(2)}, u32[]{:S(2)}) async-start(bf16[32,128,128]{2,1,0:T(8,128)(2,1)} %render0.1), calls=%async_computation.1 | async-start | bytes 2097152 | tf_op jit(solution)/shard_map/all_to_all | solution.py:251

commit v8 on v7

--- a/solution.py
+++ b/solution.py
@@ -15,7 +15,7 @@
 AXES = ("depth", "tile")
 
 
-def render_kernel(slope_ref, pivot_ref, owner_ref, cell_ref, order_ref, rank_ref, slab_ref, vol_ref, res_ref, out_ref, even_ref, odd_ref, ramp_ref, acc_ref, seen_ref, tint_ref, print_ref, *, view, count, tagged, tiles, bands):
+def render_kernel(slope_ref, pivot_ref, owner_ref, cell_ref, order_ref, rank_ref, slab_ref, vol_ref, res_ref, out_ref, even_ref, odd_ref, ramp_ref, acc_ref, seen_ref, tint_ref, print_ref, tag_ref, *, view, count, tagged, tiles, bands):
     step = pl.program_id(0)
     bricks = count
     edge = vol_ref.shape[1]
@@ -54,6 +54,25 @@
                     given = want.astype(jnp.bfloat16)
                     debt = want - given.astype(jnp.float32)
                     ramp_ref[j, ch, place] = given
+
+    def codes():
+        if tagged:
+            views = order_ref.shape[0]
+            slabs = rank_ref.shape[1]
+            cells_each = CELLS // slabs
+            bricks_all = slabs * tiles * count
+            lane = lax.rem(lax.broadcasted_iota(jnp.int32, (TAGS, cols), 1), views * count)
+            code = jnp.zeros((TAGS, cols), jnp.int32)
+            for v in range(views):
+                rank = rank_ref[v, slab_ref[0]]
+                for b in range(count):
+                    cell = cell_ref[v, b]
+                    group = lax.div(cell, cells_each)
+                    place = (group * tiles + owner_ref[v, b]) * cells_each + (cell - group * cells_each)
+                    value = (place * slabs + rank) * bricks_all + order_ref[v, b]
+                    code = jnp.where(lane == v * count + b, value, code)
+            digit = lax.broadcasted_iota(jnp.int32, (TAGS, cols), 0)
+            tag_ref[...] = jnp.where(digit == 0, code & 255, jnp.where(digit == 1, (code >> 8) & 255, code >> 16)).astype(jnp.float32)
 
     def march(block, samp_ref):
         for top in range(0, edge, strip):
@@ -106,6 +125,7 @@
     @pl.when(step == 0)
     def _():
         ramps()
+        codes()
         loop(lambda block: multiply(block, even_ref))
 
     for parity, (own, other) in enumerate(((even_ref, odd_ref), (odd_ref, even_ref))):
@@ -127,32 +147,14 @@
         loop(lambda block: march(block, last))
         finish(step - 1)
 
-        if tagged:
-            views = order_ref.shape[0]
-            slabs = rank_ref.shape[1]
-            cells_each = CELLS // slabs
-            bricks_all = slabs * tiles * count
-            lane = lax.rem(lax.broadcasted_iota(jnp.int32, (TAGS, cols), 1), views * count)
-            code = jnp.zeros((TAGS, cols), jnp.int32)
-            for v in range(views):
-                rank = rank_ref[v, slab_ref[0]]
-                for b in range(count):
-                    cell = cell_ref[v, b]
-                    group = lax.div(cell, cells_each)
-                    place = (group * tiles + owner_ref[v, b]) * cells_each + (cell - group * cells_each)
-                    value = (place * slabs + rank) * bricks_all + order_ref[v, b]
-                    code = jnp.where(lane == v * count + b, value, code)
-            digit = lax.broadcasted_iota(jnp.int32, (TAGS, cols), 0)
-            tags = jnp.where(digit == 0, code & 255, jnp.where(digit == 1, (code >> 8) & 255, code >> 16)).astype(jnp.float32)
-
         def swap(row, carry):
             for band in range(bands):
                 part = print_ref[pl.ds(row * bands + band, 4 * bricks, stride=pitch), :]
                 out_ref[row, band * 4 * bricks:(band + 1) * 4 * bricks, :] = part.astype(jnp.bfloat16)
             if tagged:
-                out_ref[row, bands * 4 * bricks:, :] = tags.astype(jnp.bfloat16)
+                out_ref[row, bands * 4 * bricks:, :] = tag_ref[...].astype(jnp.bfloat16)
             return carry
-        lax.fori_loop(0, edge // bands, swap, 0, unroll=2)
+        lax.fori_loop(0, edge // bands, swap, 0, unroll=8)
 
 
 def render(volume, resampler, slope, pivot, tags, view, first, count, bands, tagged):
@@ -173,13 +175,14 @@
         out_specs=pl.BlockSpec((edge // bands, slots, cols), lambda g: (0, 0, 0)),
         out_shape=jax.ShapeDtypeStruct((edge // bands, slots, cols), jnp.bfloat16),
         scratch_shapes=[
-            pltpu.VMEM((edge * pitch, cols), jnp.float32),
-            pltpu.VMEM((edge * pitch, cols), jnp.float32),
+            pltpu.VMEM(((edge + 1) * pitch, cols), jnp.float32),
+            pltpu.VMEM(((edge + 1) * pitch, cols), jnp.float32),
             pltpu.VMEM((GROUP, 3, 2, 16, cols), jnp.bfloat16),
             pltpu.VMEM((edge, cols), jnp.float32),
             pltpu.VMEM((edge, cols), jnp.float32),
             pltpu.VMEM((3, edge, cols), jnp.float32),
-            pltpu.VMEM((4 * count * pitch, cols), jnp.float32),
+            pltpu.VMEM(((4 * count + 1) * pitch, cols), jnp.float32),
+            pltpu.VMEM((TAGS, cols), jnp.float32),
         ],
         name=f"render{view}",
     )(slope, pivot, *tags, volume, resampler)

time: 112 us -> 112 us (level)
  no operation moved by 1% of the time
where the time goes in v8:
time: 112 us; the launch traced here: 111 us
  Pallas kernels  57.3 us (51%)
  waiting for transfers between devices  25.1 us (22%)
  starting transfers between devices  12.7 us (11%)
  blocking collectives  12.6 us (11%)
  local copies, waits for them, and re-layouts  2.07 us (2%)
    pallas_call x2, Pallas kernels, render(): pl.pallas_call(functools.partial(render_kernel, view=view, count=count, t...  54.1 us
    all_to_all x2, waiting for transfers between devices, exchange(): return lax.all_to_all(parts, AXES, split_axis=0, concat_axis=0, tiled=True)  25.1 us
    all_to_all x2, starting transfers between devices, exchange(): return lax.all_to_all(parts, AXES, split_axis=0, concat_axis=0, tiled=True)  12.7 us
    all_to_all x1, blocking collectives, exchange(): return lax.all_to_all(parts, AXES, split_axis=0, concat_axis=0, tiled=True)  12.6 us
    pallas_call x2, Pallas kernels, compose(): pl.pallas_call(functools.partial(compose_kernel, base=base, count=count),...  3.19 us
  transfers between devices with their start and end apart: 2, of which 2 were waited for; matrix products, arithmetic and copies ran while one was open for 1% of the time, Pallas kernels for 27%

profile of v8, /device:TPU:0, one launch (start us, length us, event | category | flops | bytes accessed | tf_op | source)
XLA Modules:
  0.0 111.4 jit_solution(11965375159391138590)
XLA Ops:
  0.6 25.7 %render1.1 = bf16[32,136,128]{2,1,0:T(8,128)(2,1)} custom-call(f32[3]{0:T(128)} %slope_ref.3, f32[3]{0:T(128)} %pivot_ref.3, s32[2,16]{1,0:T(2,128)} %bitcast.29, s32[2,16]{1,0:T(2,128)} %bitcast.31, s32[2,16]{1,0:T(2,128)} %order_ref.3, s32[2,4]{1,0:T(2,128)} %rank_ref.3, s32[1]{0:T(128)} %bitcast.2.slab_ref, bf16[16,64,64,64]{3,2,1,0:T(8,128)(2,1)} %vol_ref.3, ...), custom_call_target="tpu_custom_call" | custom-call | tf_op jit(solution)/shard_map/render1/pallas_call | solution.py:165
  26.3 7.3 %all-to-all-start = ((bf16[32,136,128]{2,1,0:T(8,128)(2,1)}), bf16[32,136,128]{2,1,0:T(8,128)(2,1)S(1)}, u32[]{:S(2)}, u32[]{:S(2)}) async-start(bf16[32,136,128]{2,1,0:T(8,128)(2,1)} %render1.1), calls=%async_computation | async-start | bytes 2228224 | tf_op jit(solution)/shard_map/all_to_all | solution.py:254
  33.6 28.4 %render0.1 = bf16[32,128,128]{2,1,0:T(8,128)(2,1)} custom-call(f32[3]{0:T(128)} %slope_ref.3, f32[3]{0:T(128)} %pivot_ref.3, s32[2,16]{1,0:T(2,128)} %bitcast.30, s32[2,16]{1,0:T(2,128)} %bitcast.32, s32[2,16]{1,0:T(2,128)} %order_ref.3, s32[2,4]{1,0:T(2,128)} %rank_ref.3, s32[1]{0:T(128)} %bitcast.2.slab_ref, bf16[16,64,64,64]{3,2,1,0:T(8,128)(2,1)} %vol_ref.3, ...), custom_call_target="tpu_custom_call" | custom-call | tf_op jit(solution)/shard_map/render0/pallas_call | solution.py:165
  62.1 0.5 all-to-all-done.got_ref
  62.5 5.4 %all-to-all-start.1 = ((bf16[32,128,128]{2,1,0:T(8,128)(2,1)}), bf16[32,128,128]{2,1,0:T(8,128)(2,1)S(1)}, u32[]{:S(2)}, u32[]{:S(2)}) async-start(bf16[32,128,128]{2,1,0:T(8,128)(2,1)} %render0.1), calls=%async_computation.1 | async-start | bytes 2097152 | tf_op jit(solution)/shard_map/all_to_all | solution.py:254
  68.0 0.1 copy.34
  68.1 0.1 copy.37
  68.1 0.1 copy.38
  68.2 0.1 stack_squeeze.14
  68.3 0.1 slice.46.row_ref
  68.4 0.1 copy.35
  68.5 0.1 stack_squeeze.12
  68.5 0.1 slice.43.row_ref
  68.6 0.1 reshape.34
  68.8 0.1 copy.40.col_ref
  68.9 0.1 copy.41.col_ref
  69.1 1.6 %compose.2.refs_0_ = f32[64,2,8,128]{3,2,1,0:T(8,128)S(1)} custom-call(s32[1,512]{1,0:T(1,128)S(1)} %slice.46.row_ref, s32[512,2]{1,0:T(8,128)S(1)} %copy.40.col_ref, bf16[32,136,128]{2,1,0:T(8,128)(2,1)S(1)} %all-to-all-done.got_ref), custom_call_target="tpu_custom_call" | custom-call | tf_op jit(solution)/shard_map/compose/pallas_call | solution.py:236
  70.7 24.7 %all-to-all-done.1.got_ref = bf16[32,128,128]{2,1,0:T(8,128)(2,1)S(1)} async-done(((bf16[32,128,128]{2,1,0:T(8,128)(2,1)}), bf16[32,128,128]{2,1,0:T(8,128)(2,1)S(1)}, u32[]{:S(2)}, u32[]{:S(2)}) %all-to-all-start.1) | async-done | bytes 1048608 | tf_op jit(solution)/shard_map/all_to_all | solution.py:254
  95.4 1.6 %compose.3 = f32[64,2,8,128]{3,2,1,0:T(8,128)S(1)} custom-call(s32[1,512]{1,0:T(1,128)S(1)} %slice.43.row_ref, s32[512,2]{1,0:T(8,128)S(1)} %copy.41.col_ref, bf16[32,128,128]{2,1,0:T(8,128)(2,1)S(1)} %all-to-all-done.1.got_ref, f32[64,2,8,128]{3,2,1,0:T(8,128)S(1)} %compose.2.refs_0_), custom_call_target="tpu_custom_call", output_to_operand_aliasing={{}: (3, {})} | custom-call | tf_op jit(solution)/shard_map/compose/pallas_call | solution.py:236
  97.0 12.6 %all_to_all.15 = f16[32,4,8,128]{3,2,1,0:T(8,128)(2,1)S(1)} all-to-all(f16[32,4,8,128]{3,2,1,0:T(8,128)(2,1)S(1)} %bitcast.25), channel_id=1, replica_groups=mesh['depth'=4,'tile'=8] {'depth','tile'}, dimensions={0} | all-to-all | bytes 524288 | tf_op jit(solution)/shard_map/all_to_all | solution.py:254
  109.6 0.1 convert.6
  109.7 0.3 copy.42
  110.0 0.8 slice_bitcast_fusion
  110.7 0.7 slice_multiply_fusion
  (9 shorter events, 0.1 us)
Async XLA Ops:
  26.3 36.2 %all-to-all-start = ((bf16[32,136,128]{2,1,0:T(8,128)(2,1)}), bf16[32,136,128]{2,1,0:T(8,128)(2,1)S(1)}, u32[]{:S(2)}, u32[]{:S(2)}) async-start(bf16[32,136,128]{2,1,0:T(8,128)(2,1)} %render1.1), calls=%async_computation | async-start | bytes 2228224 | tf_op jit(solution)/shard_map/all_to_all | solution.py:254
  62.5 32.9 %all-to-all-start.1 = ((bf16[32,128,128]{2,1,0:T(8,128)(2,1)}), bf16[32,128,128]{2,1,0:T(8,128)(2,1)S(1)}, u32[]{:S(2)}, u32[]{:S(2)}) async-start(bf16[32,128,128]{2,1,0:T(8,128)(2,1)} %render0.1), calls=%async_computation.1 | async-start | bytes 2097152 | tf_op jit(solution)/shard_map/all_to_all | solution.py:254

commit v9 on v8

--- a/solution.py
+++ b/solution.py
@@ -284,9 +284,10 @@
         made = compose(codes[view][None], col, got, made, view, views, count, bands, places, base)
     final = exchange(made.astype(jnp.float16).reshape(devices, cells_each * views, bands * 4, width))
     final = final.reshape(edge // bands, groups, cells_each, views, bands, 4, width)
-    final = final.transpose(3, 5, 2, 0, 4, 1, 6).reshape(views, 4, cells_each * edge, cols)
-    final = final.astype(jnp.float32)
-    return final[:, :3, None], jnp.square(final[:, 3:])
+    colour = final[..., :3, :].astype(jnp.float32).transpose(3, 5, 2, 0, 4, 1, 6)
+    root = final[..., 3, :].astype(jnp.float32).transpose(3, 2, 0, 4, 1, 5)
+    colour = colour.reshape(views, 3, 1, cells_each * edge, cols)
+    return colour, jnp.square(root).reshape(views, 1, cells_each * edge, cols)
 
 
 def solution(mesh):

time: 112 us -> 112 us (level)
  no operation moved by 1% of the time
where the time goes in v9:
time: 112 us
  Pallas kernels  57.3 us (51%)
  waiting for transfers between devices  25.1 us (22%)
  starting transfers between devices  12.7 us (11%)
  blocking collectives  12.6 us (11%)
  local copies, waits for them, and re-layouts  2.15 us (2%)
    pallas_call x2, Pallas kernels, render(): pl.pallas_call(functools.partial(render_kernel, view=view, count=count, t...  54.1 us
    all_to_all x2, waiting for transfers between devices, exchange(): return lax.all_to_all(parts, AXES, split_axis=0, concat_axis=0, tiled=True)  25.1 us
    all_to_all x2, starting transfers between devices, exchange(): return lax.all_to_all(parts, AXES, split_axis=0, concat_axis=0, tiled=True)  12.7 us
    all_to_all x1, blocking collectives, exchange(): return lax.all_to_all(parts, AXES, split_axis=0, concat_axis=0, tiled=True)  12.6 us
    pallas_call x2, Pallas kernels, compose(): pl.pallas_call(functools.partial(compose_kernel, base=base, count=count),...  3.19 us
  transfers between devices with their start and end apart: 2, of which 2 were waited for; matrix products, arithmetic and copies ran while one was open for 1% of the time, Pallas kernels for 27%

profile of v9, /device:TPU:0, one launch (start us, length us, event | category | flops | bytes accessed | tf_op | source)
XLA Modules:
  0.0 111.6 jit_solution(292529362678548296)
XLA Ops:
  0.6 25.7 %render1.1 = bf16[32,136,128]{2,1,0:T(8,128)(2,1)} custom-call(f32[3]{0:T(128)} %slope_ref.3, f32[3]{0:T(128)} %pivot_ref.3, s32[2,16]{1,0:T(2,128)} %bitcast.29, s32[2,16]{1,0:T(2,128)} %bitcast.31, s32[2,16]{1,0:T(2,128)} %order_ref.3, s32[2,4]{1,0:T(2,128)} %rank_ref.3, s32[1]{0:T(128)} %bitcast.2.slab_ref, bf16[16,64,64,64]{3,2,1,0:T(8,128)(2,1)} %vol_ref.3, ...), custom_call_target="tpu_custom_call" | custom-call | tf_op jit(solution)/shard_map/render1/pallas_call | solution.py:165
  26.3 7.3 %all-to-all-start = ((bf16[32,136,128]{2,1,0:T(8,128)(2,1)}), bf16[32,136,128]{2,1,0:T(8,128)(2,1)S(1)}, u32[]{:S(2)}, u32[]{:S(2)}) async-start(bf16[32,136,128]{2,1,0:T(8,128)(2,1)} %render1.1), calls=%async_computation | async-start | bytes 2228224 | tf_op jit(solution)/shard_map/all_to_all | solution.py:254
  33.6 28.4 %render0.1 = bf16[32,128,128]{2,1,0:T(8,128)(2,1)} custom-call(f32[3]{0:T(128)} %slope_ref.3, f32[3]{0:T(128)} %pivot_ref.3, s32[2,16]{1,0:T(2,128)} %bitcast.30, s32[2,16]{1,0:T(2,128)} %bitcast.32, s32[2,16]{1,0:T(2,128)} %order_ref.3, s32[2,4]{1,0:T(2,128)} %rank_ref.3, s32[1]{0:T(128)} %bitcast.2.slab_ref, bf16[16,64,64,64]{3,2,1,0:T(8,128)(2,1)} %vol_ref.3, ...), custom_call_target="tpu_custom_call" | custom-call | tf_op jit(solution)/shard_map/render0/pallas_call | solution.py:165
  62.1 0.5 all-to-all-done.got_ref
  62.5 5.4 %all-to-all-start.1 = ((bf16[32,128,128]{2,1,0:T(8,128)(2,1)}), bf16[32,128,128]{2,1,0:T(8,128)(2,1)S(1)}, u32[]{:S(2)}, u32[]{:S(2)}) async-start(bf16[32,128,128]{2,1,0:T(8,128)(2,1)} %render0.1), calls=%async_computation.1 | async-start | bytes 2097152 | tf_op jit(solution)/shard_map/all_to_all | solution.py:254
  68.0 0.1 copy.37
  68.1 0.1 copy.40
  68.1 0.1 copy.41
  68.2 0.1 stack_squeeze.14
  68.3 0.1 slice.46.row_ref
  68.4 0.1 copy.38
  68.5 0.1 stack_squeeze.12
  68.5 0.1 slice.43.row_ref
  68.6 0.1 reshape.54
  68.8 0.1 copy.43.col_ref
  68.9 0.1 copy.44.col_ref
  69.1 1.6 %compose.2.refs_0_ = f32[64,2,8,128]{3,2,1,0:T(8,128)S(1)} custom-call(s32[1,512]{1,0:T(1,128)S(1)} %slice.46.row_ref, s32[512,2]{1,0:T(8,128)S(1)} %copy.43.col_ref, bf16[32,136,128]{2,1,0:T(8,128)(2,1)S(1)} %all-to-all-done.got_ref), custom_call_target="tpu_custom_call" | custom-call | tf_op jit(solution)/shard_map/compose/pallas_call | solution.py:236
  70.7 24.7 %all-to-all-done.1.got_ref = bf16[32,128,128]{2,1,0:T(8,128)(2,1)S(1)} async-done(((bf16[32,128,128]{2,1,0:T(8,128)(2,1)}), bf16[32,128,128]{2,1,0:T(8,128)(2,1)S(1)}, u32[]{:S(2)}, u32[]{:S(2)}) %all-to-all-start.1) | async-done | bytes 1048608 | tf_op jit(solution)/shard_map/all_to_all | solution.py:254
  95.4 1.6 %compose.3 = f32[64,2,8,128]{3,2,1,0:T(8,128)S(1)} custom-call(s32[1,512]{1,0:T(1,128)S(1)} %slice.43.row_ref, s32[512,2]{1,0:T(8,128)S(1)} %copy.44.col_ref, bf16[32,128,128]{2,1,0:T(8,128)(2,1)S(1)} %all-to-all-done.1.got_ref, f32[64,2,8,128]{3,2,1,0:T(8,128)S(1)} %compose.2.refs_0_), custom_call_target="tpu_custom_call", output_to_operand_aliasing={{}: (3, {})} | custom-call | tf_op jit(solution)/shard_map/compose/pallas_call | solution.py:236
  97.0 12.6 %all_to_all.15 = f16[32,4,8,128]{3,2,1,0:T(8,128)(2,1)S(1)} all-to-all(f16[32,4,8,128]{3,2,1,0:T(8,128)(2,1)S(1)} %bitcast.23), channel_id=1, replica_groups=mesh['depth'=4,'tile'=8] {'depth','tile'}, dimensions={0} | all-to-all | bytes 524288 | tf_op jit(solution)/shard_map/all_to_all | solution.py:254
  109.6 0.1 slice_convert_fusion
  109.8 0.2 slice.59
  109.9 0.9 copy.49
  110.9 0.7 convert_multiply_fusion
  (9 shorter events, 0.1 us)
Async XLA Ops:
  26.3 36.2 %all-to-all-start = ((bf16[32,136,128]{2,1,0:T(8,128)(2,1)}), bf16[32,136,128]{2,1,0:T(8,128)(2,1)S(1)}, u32[]{:S(2)}, u32[]{:S(2)}) async-start(bf16[32,136,128]{2,1,0:T(8,128)(2,1)} %render1.1), calls=%async_computation | async-start | bytes 2228224 | tf_op jit(solution)/shard_map/all_to_all | solution.py:254
  62.5 32.9 %all-to-all-start.1 = ((bf16[32,128,128]{2,1,0:T(8,128)(2,1)}), bf16[32,128,128]{2,1,0:T(8,128)(2,1)S(1)}, u32[]{:S(2)}, u32[]{:S(2)}) async-start(bf16[32,128,128]{2,1,0:T(8,128)(2,1)} %render0.1), calls=%async_computation.1 | async-start | bytes 2097152 | tf_op jit(solution)/shard_map/all_to_all | solution.py:254
